TPU v7x, 32 devices: a whole 2x2x4 slice. The times are simulated.
32 devices in a mesh: group: 4 (over x, core), replica: 8 (over z, y).
Axes of the slice: x: 2, y: 2, z: 4, core: 2. Of those that a mesh axis runs over, the one named last changes fastest.
Arguments:
- activations: float32 [16, 1024, 768], P('replica', 'group'), may hold values from -6 to 6
- out_grad: float32 [16, 1024, 768], P('replica', 'group'), may hold values from -6 to 6
- picture_ids: int32 [16, 1024], P('replica'), may hold values from -1 to 9, as said below
- ln1_gain: float32 [768], P('group'), may hold values from 0.5 to 1.5
- ln1_bias: float32 [768], P('group'), may hold values from -3 to 3
- w_query: float32 [768, 768], P(None, 'group'), may hold values from -0.3125 to 0.3125
- q_bias: float32 [768], P('group'), may hold values from -3 to 3
- w_key: float32 [768, 768], P(None, 'group'), may hold values from -0.3125 to 0.3125
- w_value: float32 [768, 768], P(None, 'group'), may hold values from -0.21875 to 0.21875
- v_bias: float32 [768], P('group'), may hold values from -3 to 3
- w_out: float32 [768, 768], P('group'), may hold values from -1.75 to 1.75
- out_bias: float32 [768], P('group'), may hold values from -3 to 3
- ln2_gain: float32 [768], P('group'), may hold values from 0.5 to 1.5
- ln2_bias: float32 [768], P('group'), may hold values from -3 to 3
- w_fc1: float32 [768, 3072], P(None, 'group'), may hold values from -0.21875 to 0.21875
- fc1_bias: float32 [3072], P('group'), may hold values from -3 to 3
- w_fc2: float32 [3072, 768], P('group'), may hold values from -0.109375 to 0.109375
- fc2_bias: float32 [768], P('group'), may hold values from -3 to 3
Outputs:
- output: float32 [16, 1024, 768], P('replica', 'group')
- grad_input: float32 [16, 1024, 768], P('replica', 'group')
- grad_ln1_gain: float32 [768], P('group')
- grad_ln1_bias: float32 [768], P('group')
- grad_w_query: float32 [768, 768], P(None, 'group')
- grad_q_bias: float32 [768], P('group')
- grad_w_key: float32 [768, 768], P(None, 'group')
- grad_w_value: float32 [768, 768], P(None, 'group')
- grad_v_bias: float32 [768], P('group')
- grad_w_out: float32 [768, 768], P('group')
- grad_out_bias: float32 [768], P('group')
- grad_ln2_gain: float32 [768], P('group')
- grad_ln2_bias: float32 [768], P('group')
- grad_w_fc1: float32 [768, 3072], P(None, 'group')
- grad_fc1_bias: float32 [3072], P('group')
- grad_w_fc2: float32 [3072, 768], P('group')
- grad_fc2_bias: float32 [768], P('group')
Inputs may be any that keep to these rules, and one draw needn't show every extreme that they name: `picture_ids`: each row holds whole pictures numbered 0, 1, 2 and so on from its start, each of 100 to 1024 patches, followed by padding marked -1.
All inputs are finite; a program needn't handle non-finite values.
Results may differ from a plain program's by a relative error of at most 0.04.
Values may be sent and summed in bfloat16 or wider, within the bound.
No kernel may reach another device: no remote copies, remote signals or barrier semaphores. Data moves between devices by JAX's collectives and lax.ppermute only.
A program may use at most 256 MiB of HBM per device.

v0:
```python
import jax
import jax.numpy as jnp
from jax import lax
from jax.experimental import pallas as pl
from jax.experimental.pallas import tpu as pltpu
from jax.sharding import PartitionSpec as P

HEAD_DIM = 64
EPS = 1e-06
MASKED = -1e30
BF = jnp.bfloat16
F32 = jnp.float32
LANES = 128
LOG2_E = 1.4426950408889634
GELU_A = 0.7978845608028654
GELU_B = 0.044715
BLOCK = 256


def to_float(values):
    return values.astype(F32)


def dot_nn(left, right):
    return jnp.dot(left, right, preferred_element_type=F32)


def dot_nt(left, right):
    return lax.dot_general(left, right, (((1,), (1,)), ((), ())), preferred_element_type=F32)


def dot_tn(left, right):
    return lax.dot_general(left, right, (((0,), (0,)), ((), ())), preferred_element_type=F32)


def normalize(values):
    centred = values - jnp.mean(values, axis=-1, keepdims=True)
    inverse = lax.rsqrt(jnp.mean(centred * centred, axis=-1, keepdims=True) + EPS)
    return (centred * inverse, inverse)


def norm_back(grad_hat, normed_hat, inverse):
    return inverse * (
        grad_hat
        - jnp.mean(grad_hat, axis=-1, keepdims=True)
        - normed_hat * jnp.mean(grad_hat * normed_hat, axis=-1, keepdims=True)
    )


def column_sum(values):
    return jnp.sum(to_float(values), axis=0, keepdims=True)


def shape(dims, dtype):
    return jax.ShapeDtypeStruct(dims, dtype)


def after(value, *others):
    return lax.optimization_barrier((value, *others))[0]


SEQUENCE = (
    "W1", "R", "W0", "m", "N", "B0", "m", "B1", "m", "A1",
    "A0", "a", "m", "I1", "I0", "G", "m", "F", "C", "U",
    "a", "m", "a", "L",
)
COSTS = {
    "project": 8000000000,
    "attend_1": 8000000000,
    "attend_0": 8000000000,
    "mlp_0": 8000000000,
    "mlp_1": 8000000000,
    "mlp_kept": 6000000000,
    "attend_back_0": 6000000000,
}
MLP_GROUPS = (1, 1)
ATT_GROUPS = (1, 1)
RS4_EARLY = True
ORDER = []
IN_VMEM = pl.BlockSpec(memory_space=pltpu.VMEM)


def launch(body, name, ins, outs, grid=(1,), scratch=(), aliases=None, flops=0, exps=0, scalar=None, limit=12):
    ins = list(ins)
    if ORDER:
        sizes = [(a.size if spec is None else a.size * 1024, i) for i, (a, spec) in enumerate(ins)]
        at = min(sizes)[1]
        ins[at] = (after(ins[at][0], ORDER[0]), ins[at][1])
    in_specs = [IN_VMEM if spec is None else spec for _, spec in ins]
    out_specs = [IN_VMEM if spec is None else spec for _, spec in outs]
    arrays = [
        a if spec is None else pltpu.with_memory_space_constraint(a, pltpu.HBM) for a, spec in ins
    ]
    count = 0
    if scalar is not None:
        arrays, count = [scalar] + arrays, 1
    results = pl.pallas_call(
        body,
        grid_spec=pltpu.PrefetchScalarGridSpec(
            num_scalar_prefetch=count,
            grid=grid,
            in_specs=in_specs,
            out_specs=out_specs,
            scratch_shapes=list(scratch),
        ),
        input_output_aliases=aliases or {},
        out_shape=[o if spec is None else pltpu.HBM(o.shape, o.dtype) for o, spec in outs],
        cost_estimate=pl.CostEstimate(
            flops=COSTS.get(name, 1), transcendentals=0, bytes_accessed=1
        ),
        compiler_params=pltpu.CompilerParams(vmem_limit_bytes=limit << 20),
        name=name,
    )(*arrays)
    ORDER[:] = [min(results, key=lambda a: a.size)]
    return results


def step_rows(size=BLOCK):
    return pl.ds(pl.multiple_of(pl.program_id(0) * size, size), size)


def held(*dims):
    return pl.BlockSpec(dims, lambda *_: (0,) * len(dims), pipeline_mode=pl.Buffered(1))


def by_step(*dims):
    return pl.BlockSpec(dims, lambda i, *_: (i,) + (0,) * (len(dims) - 1))


def row_spec(quarter, width, other):
    return pl.BlockSpec(
        (None, quarter, width), lambda i, c: ((1 - c[0]) if other else c[0], 0, 0)
    )


def split_inputs(activations, small, position, shard, padded):
    _, quarter, width = activations.shape
    extra = 16

    def body(at_ref, own_in, other_ref, small_ref, chip_ref, diagonal_ref, partner_ref, mine_ref):
        lane = lax.broadcasted_iota(jnp.int32, (1, width), 1)
        low = at_ref[1] * shard
        inside = (lane >= low) & (lane < low + shard)
        wide = jnp.concatenate([small_ref[0:6]] * (width // shard), axis=1)
        placed = jnp.where(inside, wide, 0.0).astype(BF)
        gap = jnp.zeros((1, padded - shard), F32)
        query_value = jnp.concatenate(
            [small_ref[6:7], gap, jnp.zeros((1, padded), F32), small_ref[7:8], gap], axis=1
        )
        hidden = jnp.concatenate([small_ref[8 + i : 9 + i] for i in range(4)], axis=1)
        rest = jnp.zeros((extra - 8, width), F32)
        mine = jnp.concatenate([to_float(placed), query_value, hidden, rest], axis=0)
        mine = to_float(mine.astype(BF))
        mine_ref[...] = mine
        chip_ref[:quarter] = own_in[...].astype(BF)
        chip_ref[quarter:] = mine.astype(BF)
        diagonal_ref[:quarter] = other_ref[...].astype(BF)
        diagonal_ref[quarter:] = mine.astype(BF)
        partner_ref[:quarter] = other_ref[...]
        partner_ref[quarter:] = mine

    dims = (quarter + extra, width)
    return launch(
        body,
        "split_inputs",
        [
            (activations, row_spec(quarter, width, False)),
            (activations, row_spec(quarter, width, True)),
            (small, None),
        ],
        [(shape(dims, BF), None)] * 2
        + [(shape(dims, F32), None), (shape((extra, width), F32), None)],
        scalar=position,
    )


def split_grads(out_grad, ids, core):
    _, quarter, width = out_grad.shape

    def body(core_ref, own_in, other_in, own_id, other_id, chip, diagonal, keep_ref, partner_ref):
        own = jnp.where(own_id[...] >= 0, own_in[...], 0.0)
        other = jnp.where(other_id[...] >= 0, other_in[...], 0.0)
        chip[...] = own.astype(BF)
        diagonal[...] = other.astype(BF)
        keep_ref[...] = own
        partner_ref[...] = other

    return launch(
        body,
        "split_grads",
        [
            (out_grad, row_spec(quarter, width, False)),
            (out_grad, row_spec(quarter, width, True)),
            (ids, row_spec(quarter, 1, False)),
            (ids, row_spec(quarter, 1, True)),
        ],
        [(shape((quarter, width), BF), None)] * 2
        + [(shape((quarter, width), F32), held(quarter, width)), (shape((quarter, width), F32), None)],
        scalar=core,
    )


def pack_attention(w_query, w_key, w_value, w_out):
    shard, width = w_out.shape
    padded = -(-shard // LANES) * LANES

    def body(q_ref, k_ref, v_ref, o_ref, out_ref):
        for i, ref in enumerate((q_ref, k_ref, v_ref, o_ref)):
            out_ref[i * padded : i * padded + shard] = ref[...].astype(BF)
            out_ref[i * padded + shard : (i + 1) * padded] = jnp.zeros((padded - shard, width), BF)

    full = pl.BlockSpec((shard, width), lambda i: (0, 0))
    return launch(
        body,
        "pack_attention",
        [(w_query.T, full), (w_key.T, full), (w_value.T, full), (w_out, full)],
        [(shape((4 * padded, width), BF), None)],
    )[0]


def pack_mlp(w_fc1, w_fc2):
    rows, columns = w_fc1.shape

    def body(up_ref, down_ref, up_out, down_out):
        at = step_rows(rows // 4)
        up_out[at] = up_ref[...].astype(BF)
        down_out[at] = down_ref[...].astype(BF)

    block = pl.BlockSpec((rows // 4, columns), lambda i: (i, 0))
    return launch(
        body,
        "pack_mlp",
        [(w_fc1, block), (w_fc2, block)],
        [(shape((rows, columns), BF), None)] * 2,
        grid=(4,),
    )


def project(activations, mine, pieces, weights, padded, core):
    _, quarter, width = activations.shape
    length = 4 * quarter
    columns = 3 * padded

    def body(core_ref, own, mine_ref, second, third, fourth, w_0, w_1, *outs):
        normed_ref, hat_ref, sides_ref, out_w, vec_ref, bias_ref, values = outs
        step = pl.program_id(0)
        pieces = (second, third, fourth)

        @pl.when(step == 0)
        def _():
            vec_ref[...] = mine_ref[0:6] + sum(
                to_float(ref[quarter : quarter + 6]) for ref in pieces
            )
            bias_ref[0:2] = mine_ref[6:8]
            bias_ref[2:4] = second[quarter + 6 : quarter + 8]
            out_w[0] = w_0[columns:]
            out_w[1] = w_1[columns:]
            values[...] = own[...]

        for i, piece in enumerate(pieces):

            @pl.when(step == i + 1)
            def _():
                values[...] = to_float(piece[:quarter])

        rows = step_rows(quarter)
        hat, _ = normalize(values[...])
        normed = (hat * vec_ref[0:1] + vec_ref[1:2]).astype(BF)
        normed_ref[...] = normed
        hat_ref[...] = hat.astype(BF)
        for side, w_ref in enumerate((w_0, w_1)):
            bias = bias_ref[2 * side : 2 * side + 1]
            sides_ref[side, rows] = (dot_nt(normed, w_ref[:columns]) + bias).astype(BF)

    return launch(
        body,
        "project",
        [(activations, row_spec(quarter, width, False))]
        + [(a, None) for a in (mine, *pieces, *weights)],
        [(shape((length, width), BF), by_step(quarter, width))] * 2
        + [(shape((2, length, columns), BF), None), (shape((2, padded, width), BF), None)]
        + [(shape((6, width), F32), None), (shape((4, width), F32), None)],
        grid=(4,),
        scratch=[pltpu.VMEM((quarter, width), F32)],
        scalar=core,
        flops=2 * length * width * 2 * columns,
    )


def lane_half():
    return lax.broadcasted_iota(jnp.int32, (1, LANES), 1) < HEAD_DIM


def head_place(head, first):
    block = slice((head // 2) * LANES, (head // 2 + 1) * LANES)
    return block, (first if head % 2 == 0 else ~first)


def attend(sides, marks, out_w, half_index, heads, dtype):
    _, length, columns = sides.shape
    padded, width = out_w.shape[1:]
    half = length // 2

    def body(sides, marks, w_ref, att_ref, inv_ref, e_ref, branch_ref, total_ref):
        side = pl.program_id(1)
        first = lane_half()
        here = step_rows()
        start = half_index * half + pl.program_id(0) * BLOCK
        rows = pl.ds(pl.multiple_of(start, BLOCK), BLOCK)
        mark_q = marks[rows, :LANES]
        mark_k = marks[:, LANES:]
        att = [jnp.zeros((BLOCK, LANES), F32)] * (padded // LANES)
        inv = list(att)
        for head in range(heads):
            block, lanes = head_place(head, first)
            scaled = to_float(sides[side, rows, block]) * (HEAD_DIM**-0.5 * LOG2_E)
            high = scaled.astype(BF)
            low = (scaled - to_float(high)).astype(BF)
            keys = sides[side, :, padded + block.start : padded + block.stop]
            left = jnp.concatenate(
                [jnp.where(lanes, high, mark_q), jnp.where(lanes, low, jnp.zeros_like(low))],
                axis=1,
            )
            right = jnp.concatenate([jnp.where(lanes, keys, mark_k), keys], axis=1)
            scores = dot_nt(left, right)
            exponent = jnp.exp2(scores - jnp.max(scores, axis=1, keepdims=True)).astype(BF)
            e_ref[head] = exponent
            values = sides[side, :, 2 * padded + block.start : 2 * padded + block.stop]
            both = dot_nn(exponent, jnp.concatenate([values, jnp.ones_like(values)], axis=1))
            inverse = 1.0 / both[:, LANES:]
            index = head // 2
            att[index] = jnp.where(lanes, both[:, :LANES] * inverse, att[index])
            inv[index] = jnp.where(lanes, inverse, inv[index])
        attended = jnp.concatenate(att, axis=1).astype(BF)
        att_ref[...] = attended
        inv_ref[...] = jnp.concatenate(inv, axis=1)
        part = dot_nn(attended, w_ref[side])

        @pl.when(side == 0)
        def _():
            total_ref[...] = part

        @pl.when(side == 1)
        def _():
            branch_ref[here] = (total_ref[...] + part).astype(dtype)

    block = pl.BlockSpec((None, BLOCK, padded), lambda i, j: (j, i, 0))
    return launch(
        body,
        f"attend_{half_index}",
        [(a, None) for a in (sides, marks, out_w)],
        [
            (shape((2, half, padded), BF), block),
            (shape((2, half, padded), F32), block),
            (
                shape((2 * heads, half, length), BF),
                pl.BlockSpec((heads, BLOCK, length), lambda i, j: (j, i, 0)),
            ),
            (shape((half, width), dtype), None),
        ],
        grid=(half // BLOCK, 2),
        scratch=[pltpu.VMEM((BLOCK, width), F32)],
        flops=8 * 2 * heads * half * length * 256,
        exps=2 * heads * half * length,
        limit=16,
    )


def second_norm(activations, core_piece, branch, received, vectors, core):
    half, width = branch.shape
    quarter = half // 2
    size = quarter // 2

    def body(core_ref, own, core_piece, branch_ref, recv_ref, vec, middle_ref, normed_ref, values):
        step = pl.program_id(0)
        here = step_rows(size)

        @pl.when(step < 2)
        def _():
            values[...] = own[...]

        @pl.when(step >= 2)
        def _():
            values[...] = core_piece[pl.ds(pl.multiple_of((step - 2) * size, size), size)]

        middle = values[...] + (branch_ref[here] + to_float(recv_ref[here]) + vec[2:3])
        middle_ref[...] = middle
        hat, _ = normalize(middle)
        normed_ref[here] = (hat * vec[3:4] + vec[4:5]).astype(BF)

    own_spec = pl.BlockSpec((None, size, width), lambda i, c: (c[0], jnp.minimum(i, 1), 0))
    return launch(
        body,
        "second_norm",
        [(activations, own_spec)] + [(a, None) for a in (core_piece, branch, received, vectors)],
        [(shape((half, width), F32), by_step(size, width)), (shape((half, width), BF), None)],
        grid=(4,),
        scratch=[pltpu.VMEM((size, width), F32)],
        scalar=core,
    )


def stack_weights(own, partner):
    def body(*refs):
        refs[4][0], refs[4][1] = refs[0][...], refs[1][...]
        refs[5][0], refs[5][1] = refs[2][...], refs[3][...]

    return launch(
        body,
        "stack_weights",
        [(a, None) for pair in zip(own, partner) for a in pair],
        [(shape((2, *a.shape), BF), None) for a in own],
    )


def mlp(normed, grad, ups, downs, bias, half_index, dtype, previous):
    rows, width = normed.shape
    hidden_size = ups.shape[2]

    def body(n_ref, g_0, g_1, up, down, bias, *rest):
        act_ref, hid_ref, out_ref, grad_ref, sum_ref, *totals = rest[len(previous) :]
        side = pl.program_id(1)
        start = half_index * rows + pl.program_id(0) * BLOCK
        shared = pl.ds(pl.multiple_of(start, BLOCK), BLOCK)

        @pl.when((pl.program_id(0) == 0) & (side == 0))
        def _():
            sum_ref[...] = jnp.zeros_like(sum_ref)

        here = step_rows()
        grad_rows = jnp.where(pl.program_id(0) == 0, g_0[...].astype(BF), g_1[...].astype(BF))
        normed_rows = n_ref[here]
        hidden = dot_nn(normed_rows, up[side]) + jnp.where(side == 0, bias[1:2], bias[3:4])
        grad_act = dot_nt(grad_rows, down[side])
        square = hidden * hidden
        th = jnp.tanh(hidden * (GELU_A + GELU_A * GELU_B * square))
        gate = 0.5 + 0.5 * th
        act = (hidden * gate).astype(BF)
        slope = gate + (0.5 * hidden) * (1.0 - th * th) * (GELU_A + 3.0 * GELU_A * GELU_B * square)
        grad_hidden = (grad_act * slope).astype(BF)
        act_ref[side, shared] = act
        hid_ref[side, shared] = grad_hidden
        sum_ref[side] += column_sum(grad_hidden)
        out = dot_nn(act, down[side])
        grad_in = dot_nt(grad_hidden, up[side])

        if dtype == F32:

            @pl.when(side == 0)
            def _():
                out_ref[...] = out
                grad_ref[...] = grad_in

            @pl.when(side == 1)
            def _():
                out_ref[...] += out
                grad_ref[...] += grad_in

        else:

            @pl.when(side == 0)
            def _():
                totals[0][...] = out
                totals[1][...] = grad_in

            @pl.when(side == 1)
            def _():
                out_ref[here] = (totals[0][...] + out).astype(dtype)
                grad_ref[here] = (totals[1][...] + grad_in).astype(dtype)

    return launch(
        body,
        f"mlp_{half_index}",
        [(a, None) for a in (normed, *grad, ups, downs, bias, *previous)],
        [(shape((2, 2 * rows, hidden_size), BF), None)] * 2
        + [(shape((rows, width), dtype), by_step(BLOCK, width) if dtype == F32 else None)] * 2
        + [(shape((2, 1, hidden_size), F32), None)],
        grid=(rows // BLOCK, 2),
        scratch=[] if dtype == F32 else [pltpu.VMEM((BLOCK, width), F32)] * 2,
        aliases={6 + i: i for i in range(len(previous))},
        flops=8 * rows * width * 2 * hidden_size,
        exps=rows * 2 * hidden_size,
        limit=12,
    )


def second_norm_back(middle, grad, received, grad_own, grad_partner, vectors):
    quarter, width = grad_own.shape
    size = quarter // 2

    def body(
        middle_ref, grad_ref, recv_ref, own, partner, vec, out_ref, branch_ref, sum_ref, values
    ):
        step = pl.program_id(0)
        here = step_rows(size)

        @pl.when(step < 2)
        def _():
            values[...] = own[...]

        @pl.when(step >= 2)
        def _():
            values[...] = partner[pl.ds(pl.multiple_of((step - 2) * size, size), size)]

        hat, inverse = normalize(middle_ref[...])
        incoming = grad_ref[...] + to_float(recv_ref[here])
        out = values[...] + norm_back(incoming * vec[3:4], hat, inverse)
        branch = out.astype(BF)
        out_ref[...] = out
        branch_ref[here] = branch
        sums = jnp.concatenate(
            [
                column_sum(incoming * hat),
                column_sum(incoming),
                column_sum(branch),
                column_sum(values[...].astype(BF)),
            ],
            axis=0,
        )

        @pl.when(step == 0)
        def _():
            sum_ref[...] = sums

        @pl.when(step > 0)
        def _():
            sum_ref[...] += sums

    dims = (2 * quarter, width)
    own_spec = pl.BlockSpec((size, width), lambda i: (jnp.minimum(i, 1), 0))
    return launch(
        body,
        "second_norm_back",
        [(middle, by_step(size, width)), (grad, by_step(size, width)), (received, None)]
        + [(grad_own, own_spec), (grad_partner, None), (vectors, None)],
        [
            (shape(dims, F32), by_step(size, width)),
            (shape(dims, BF), None),
            (shape((4, width), F32), None),
        ],
        grid=(4,),
        scratch=[pltpu.VMEM((size, width), F32)],
    )


def mlp_weight_grad(normed, grads, activated, hidden, side):
    rows, width = normed[0].shape
    size = hidden.shape[2]

    def body(n_0, n_1, g_0, g_1, g_2, g_3, act_ref, hid_ref, out_ref):
        first, second = slice(0, rows), slice(rows, 2 * rows)
        up = dot_tn(n_0[...], hid_ref[side, first]) + dot_tn(n_1[...], hid_ref[side, second])
        out_ref[:width] = up.astype(BF)
        down, at = None, rows // 2
        for i, ref in enumerate((g_0, g_1, g_2, g_3)):
            part = dot_tn(act_ref[side, i * at : (i + 1) * at], ref[...].astype(BF))
            down = part if down is None else down + part
        out_ref[width:] = down.astype(BF)

    dims = (width + size, width)
    return launch(
        body,
        ("mlp_kept", "mlp_sent")[side],
        [(a, None) for a in (*normed, *grads, activated, hidden)],
        [(shape(dims, BF), None)],
        flops=8 * rows * width * size,
        limit=14,
    )[0]


def attend_back(grad, out_w, attended, inverse, exponent, sides, half_index, heads, previous, only=None):
    _, length, columns = sides.shape
    padded = columns // 3
    half, width = grad.shape
    last = previous is not None
    steps = half // BLOCK

    def body(grad_ref, w_ref, at_ref, inv_ref, sides, e_ref, *rest):
        if last:
            dk_in, dv_in, dq_ref, dk_out, dv_out, dk_sum, dv_sum = rest
        else:
            dq_ref, dk_sum, dv_sum = rest
        step = pl.program_id(0)
        side = pl.program_id(1) if only is None else only
        slot = side if only is None else 0
        here = step_rows()
        rows = pl.ds(pl.multiple_of(half_index * half + step * BLOCK, BLOCK), BLOCK)

        @pl.when(step == 0)
        def _():
            dk_sum[slot] = dk_in[side] if last else jnp.zeros((length, padded), F32)
            dv_sum[slot] = dv_in[side] if last else jnp.zeros((length, padded), F32)

        first = lane_half()
        lane = lax.broadcasted_iota(jnp.int32, (1, LANES), 1)
        zero = jnp.zeros((), BF)
        grad_att = to_float(dot_nt(grad_ref[here], w_ref[side]).astype(BF))
        scaled = (grad_att * inv_ref[...]).astype(BF)
        product = to_float(scaled) * to_float(at_ref[...])
        dq = [None] * (padded // LANES)
        for head in range(heads):
            block, lanes = head_place(head, first)
            keys = sides[side, :, padded + block.start : padded + block.stop]
            values = sides[side, :, 2 * padded + block.start : 2 * padded + block.stop]
            grad_head = jnp.where(lanes, scaled[:, block], zero)
            centre = -jnp.sum(jnp.where(lanes, product[:, block], 0.0), axis=1, keepdims=True)
            high = centre.astype(BF)
            low = (centre - to_float(high)).astype(BF)
            extra = jnp.where(lane == 0, high, jnp.where(lane == 1, low, zero))
            grad_probs = dot_nt(
                jnp.concatenate([grad_head, extra], axis=1),
                jnp.concatenate([values, jnp.ones_like(values)], axis=1),
            )
            probs = e_ref[head]
            grad_scores = (to_float(probs) * grad_probs).astype(BF)
            part = dot_nn(grad_scores, jnp.where(lanes, keys, zero))
            index = head // 2
            dq[index] = part if dq[index] is None else dq[index] + part
            queries = jnp.where(lanes, sides[side, rows, block], zero)
            dk_sum[slot, :, block] += dot_tn(grad_scores, queries)
            dv_sum[slot, :, block] += dot_tn(probs, grad_head)
        dq_ref[slot, here] = (jnp.concatenate(dq, axis=1) * HEAD_DIM**-0.5).astype(BF)

        if last:

            @pl.when(step == steps - 1)
            def _():
                dk_out[slot] = (dk_sum[slot] * HEAD_DIM**-0.5).astype(BF)
                dv_out[slot] = dv_sum[slot].astype(BF)

    count = 2 if only is None else 1
    block = pl.BlockSpec((None, BLOCK, padded), lambda i, j: (j if only is None else only, i, 0))
    ins = [(grad, None), (out_w, None), (attended, block), (inverse, block), (sides, None)]
    ins += [(exponent, pl.BlockSpec((heads, BLOCK, length), lambda i, j: (j if only is None else only, i, 0)))]
    if last:
        ins += [(a, None) for a in previous]
    sum_dtype = BF if last else F32
    return launch(
        body,
        f"attend_back_{half_index}" + ("" if only is None else f"_{only}"),
        ins,
        [(shape((count, half, padded), BF), None)]
        + [(shape((count, length, padded), sum_dtype), None)] * 2,
        grid=(steps, count),
        scratch=[pltpu.VMEM((count, length, padded), F32)] * 2 if last else [],
        flops=16 * 2 * heads * half * length * 256,
        limit=20,
    )


def input_grad(queries, keys, values, weights, hat, half_index, dtype):
    half, padded = queries[0].shape
    width = hat.shape[1]

    def body(q_0, q_1, k_0, k_1, v_0, v_1, w_0, w_1, hat_ref, out_ref, sum_ref):
        rows = slice(half_index * half, (half_index + 1) * half)
        total = None
        for w_ref, q_ref, k_ref, v_ref in ((w_0, q_0, k_0, v_0), (w_1, q_1, k_1, v_1)):
            left = jnp.concatenate([q_ref[...], k_ref[rows], v_ref[rows]], axis=1)
            part = dot_nn(left, w_ref[: 3 * padded])
            total = part if total is None else total + part
        out_ref[...] = total.astype(dtype)
        sums = [column_sum(total * to_float(hat_ref[...])), column_sum(total)]
        sum_ref[...] = jnp.concatenate(sums, axis=0)

    return launch(
        body,
        f"input_grad_{half_index}",
        [(a, None) for a in (*queries, *keys, *values, *weights)]
        + [(hat, pl.BlockSpec((half, width), lambda i: (half_index, 0)))],
        [
            (shape((half, width), dtype), held(half, width) if dtype == F32 else None),
            (shape((2, width), F32), None),
        ],
        flops=2 * half * 6 * padded * width,
    )


def attention_weight_grad(attended, grads, queries, keys, values, normed, shard, side):
    half, padded = queries[0].shape
    width = normed.shape[1]

    def body(at_0, at_1, g_0, g_1, q_0, q_1, k_ref, v_ref, n_ref, out_ref):
        n_0, n_1 = n_ref[:half], n_ref[half:]
        products = [
            dot_tn(at_0[...], g_0[...]) + dot_tn(at_1[...], g_1[...]),
            dot_tn(q_0[...], n_0) + dot_tn(q_1[...], n_1),
            dot_tn(k_ref[...], n_ref[...]),
            dot_tn(v_ref[...], n_ref[...]),
        ]
        for i, part in enumerate(products):
            out_ref[i * shard : (i + 1) * shard] = part[:shard].astype(BF)

    at_spec = pl.BlockSpec((None, half, padded), lambda i: (side, 0, 0))
    dims = (4 * shard, width)
    return launch(
        body,
        ("attention_kept", "attention_sent")[side],
        [(a, at_spec) for a in attended]
        + [(a, None) for a in (*grads, *queries, keys, values)]
        + [(normed, held(*normed.shape))],
        [(shape(dims, BF), None)],
        flops=2 * 2 * half * 4 * padded * width,
        limit=14,
    )[0]


def small_grads(norm_0, norm_1, late, queries, values, up_0, up_1):
    width = late.shape[1]
    padded = values[0].shape[1]

    def body(norm_0, norm_1, late, *rest):
        queries, values, (up_0, up_1, wide_ref, bias_ref) = rest[:4], rest[4:6], rest[6:]
        wide_ref[...] = jnp.concatenate([norm_0[...] + norm_1[...], late[...]], axis=0).astype(BF)
        for side in range(2):
            bias = [
                column_sum(queries[side][...]) + column_sum(queries[2 + side][...]),
                column_sum(values[side][...]),
                jnp.zeros((1, width - 2 * padded), F32),
            ]
            both = [jnp.concatenate(bias, axis=1), up_0[side] + up_1[side]]
            bias_ref[2 * side : 2 * side + 2] = jnp.concatenate(both, axis=0)

    return launch(
        body,
        "small_grads",
        [(a, None) for a in (norm_0, norm_1, late, *queries, *values, up_0, up_1)],
        [(shape((6, width), BF), None), (shape((4, width), F32), None)],
    )


def small_chip(wide, received, bias):
    width = wide.shape[1]

    def body(wide_ref, recv_ref, bias_ref, own_ref, sent_ref):
        total = to_float(wide_ref[...]) + to_float(recv_ref[...])
        own_ref[...] = jnp.concatenate([total, bias_ref[0:2]], axis=0)
        sent_ref[...] = jnp.concatenate([total, bias_ref[2:4]], axis=0)

    return launch(
        body,
        "small_chip",
        [(wide, None), (received, None), (bias, None)],
        [(shape((8, width), F32), None)] * 2,
    )


def small_sum(own, received):
    def body(own_ref, recv_ref, out_ref):
        out_ref[...] = (own_ref[...] + recv_ref[...]).astype(BF)

    return launch(
        body, "small_sum", [(own, None), (received, None)], [(shape(own.shape, BF), None)]
    )[0]


def home_spec(quarter, width):
    return pl.BlockSpec((None, quarter, width), lambda i, c: (c[0], 0, 0))


def first_norm_back(activations, core_piece, grad_middle, grad, received, vectors, core):
    half, width = grad.shape
    quarter = half // 2

    def body(core_ref, own, core_piece, middle_ref, grad_ref, recv_ref, vec, home_ref, sent_ref):
        for i, piece in enumerate((own, core_piece)):
            rows = slice(i * quarter, (i + 1) * quarter)
            hat, inverse = normalize(piece[:quarter])
            incoming = grad_ref[rows] + to_float(recv_ref[rows])
            out = middle_ref[rows] + norm_back(incoming * vec[0:1], hat, inverse)
            (home_ref, sent_ref)[i][...] = out

    return launch(
        body,
        "first_norm_back",
        [(activations, row_spec(quarter, width, False)), (core_piece, None)]
        + [(grad_middle, held(half, width)), (grad, held(half, width))]
        + [(received, None), (vectors, None)],
        [
            (shape((2, quarter, width), F32), home_spec(quarter, width)),
            (shape((quarter, width), F32), None),
        ],
        scalar=core,
    )


def finish_output(middle, out, received, vectors, core):
    half, width = middle.shape
    quarter = half // 2

    def body(core_ref, middle_ref, out_ref, recv_ref, vec, home_ref, sent_ref):
        total = middle_ref[...] + (out_ref[...] + to_float(recv_ref[...]) + vec[5:6])
        home_ref[...] = total[:quarter]
        sent_ref[...] = total[quarter:]

    return launch(
        body,
        "finish_output",
        [(middle, held(half, width)), (out, held(half, width)), (received, None), (vectors, None)],
        [
            (shape((2, quarter, width), F32), home_spec(quarter, width)),
            (shape((quarter, width), F32), None),
        ],
        scalar=core,
    )


def swap(values, axis, size, bit):
    return lax.ppermute(values, axis, [(i, i ^ bit) for i in range(size)])


def core_swap(values):
    return swap(values, "group", 4, 1)


def chip_swap(values):
    return swap(values, "group", 4, 2)


def diagonal_swap(values):
    return swap(values, "group", 4, 3)


def divide(kept, received, mine, count, fresh):
    rows, width = kept.shape
    part = rows // count
    total = len(received)

    def body(mine_ref, kept_ref, *refs):
        recv_refs, out_refs = refs[:total], refs[total:]
        for k in range(count):
            at = pl.ds(pl.multiple_of((mine_ref[0] ^ k) * part, 8), part)
            value = to_float(kept_ref[at])
            for ref in recv_refs:
                value = value + to_float(ref[at])
            out_refs[k][...] = value.astype(BF)

    return launch(
        body,
        "divide",
        [(kept, None if fresh else held(rows, width))] + [(a, None) for a in received],
        [(shape((part, width), BF), held(part, width))] + [(shape((part, width), BF), None)] * (count - 1),
        scalar=mine,
    )


def add_all(kept, received, extra):
    rows, width = kept.shape
    below = extra.shape[0] if extra is not None else 0

    def body(kept_ref, *refs):
        out_ref = refs[-1]
        value = to_float(kept_ref[...])
        for ref in refs[: len(received)]:
            value = value + to_float(ref[...])
        out_ref[:rows] = value.astype(BF)
        if below:
            out_ref[rows:] = refs[-2][...]

    return launch(
        body,
        "add_all",
        [(kept, held(rows, width))]
        + [(a, None) for a in received]
        + ([(extra, None)] if below else []),
        [(shape((rows + below, width), BF), None)],
    )[0]


def join(parts, mine, extra):
    rows, width = parts[0].shape
    part, count = rows - extra, len(parts)

    def body(mine_ref, *refs):
        out_ref = refs[-1]
        for k in range(count):
            at = pl.ds(pl.multiple_of((mine_ref[0] ^ k) * part, 8), part)
            out_ref[at] = refs[k][:part]
        if extra:
            out_ref[count * part :] = sum(to_float(ref[part:]) for ref in refs[:-1]).astype(BF)

    return launch(
        body,
        "join",
        [(a, None) for a in parts],
        [(shape((count * part + extra, width), BF), None)],
        scalar=mine,
    )[0]


def join_weights(parts, mine, shard, extra):
    rows, width = parts[0].shape
    part, count = rows - extra, len(parts)

    def body(mine_ref, *refs):
        total, outs = refs[-1], refs[count : count + 5]
        for k in range(count):
            at = pl.ds(pl.multiple_of((mine_ref[0] ^ k) * part, 8), part)
            total[at] = to_float(refs[k][:part])
        for i in range(4):
            outs[i][...] = total[i * shard : (i + 1) * shard]
        outs[4][...] = sum(to_float(ref[part:]) for ref in refs[:count])

    return launch(
        body,
        "join_weights",
        [(a, None) for a in parts],
        [(shape((shard, width), F32), held(shard, width))] * 4 + [(shape((extra, width), F32), None)],
        scratch=[pltpu.VMEM((count * part, width), F32)],
        scalar=mine,
    )


def join_mlp(parts, mine):
    def body(mine_ref, first_ref, second_ref, up_ref, down_ref):
        for ref, which in ((first_ref, mine_ref[0]), (second_ref, 1 - mine_ref[0])):
            for index, out_ref in enumerate((up_ref, down_ref)):

                @pl.when(which == index)
                def _():
                    out_ref[...] = to_float(ref[...])

    dims = parts[0].shape
    return launch(
        body,
        "join_mlp",
        [(a, None) for a in parts],
        [(shape(dims, F32), held(*dims))] * 2,
        scalar=mine,
    )


class ReplicaSum:
    def __init__(self, kept, received, size, first, others):
        self.kept, self.received, self.size = kept, [received], size
        self.groups, bit, bits = [], 1, size.bit_length() - 1
        while bit < size:
            take = min(first if bit == 1 else others, bits)
            self.groups.append((bit, 1 << take))
            bit, bits = bit << take, bits - take
        self.at, self.rows = 0, None

    def mine(self):
        bit, count = self.groups[self.at]
        return (lax.axis_index("replica") // bit) % count

    def exchange(self, values, k):
        bit, _ = self.groups[self.at]
        return swap(values, "replica", self.size, k * bit)

    def divide(self):
        _, count = self.groups[self.at]
        mine = self.mine().astype(jnp.int32)
        part = self.kept.shape[0] // count
        if part % 8 == 0:
            parts = divide(self.kept, self.received, mine.reshape(1), count, self.at == 0)
        else:
            value = to_float(self.kept)
            for received in self.received:
                value = value + to_float(received)
            parts = [
                lax.dynamic_slice_in_dim(value, (mine ^ k) * part, part, 0).astype(BF)
                for k in range(count)
            ]
        self.kept, self.sent = parts[0], parts[1:]

    def send(self):
        self.received = [self.exchange(a, k + 1) for k, a in enumerate(self.sent)]
        self.at += 1

    def scatter(self):
        self.divide()
        self.send()

    def total(self, extra=None):
        while self.at < len(self.groups):
            self.scatter()
        self.extra = 0 if extra is None else extra.shape[0]
        self.rows = add_all(self.kept, self.received, extra)

    def collect(self):
        self.at -= 1
        _, count = self.groups[self.at]
        self.parts = [self.rows] + [self.exchange(self.rows, k) for k in range(1, count)]

    def combine(self, final=None):
        mine = self.mine().astype(jnp.int32)
        part = self.parts[0].shape[0] - self.extra
        if final is not None:
            self.rows = final(self.parts, mine.reshape(1))
            return
        if part % 8 == 0:
            self.rows = join(self.parts, mine.reshape(1), self.extra)
            return
        width = self.parts[0].shape[1]
        value = jnp.zeros((len(self.parts) * part, width), BF)
        for k, a in enumerate(self.parts):
            value = lax.dynamic_update_slice(value, a[:part], ((mine ^ k) * part, 0))
        below = sum(to_float(a[part:]) for a in self.parts).astype(BF)
        self.rows = jnp.concatenate([value, below], axis=0)


def per_device(
    replicas,
    activations,
    out_grad,
    picture_ids,
    ln1_gain,
    ln1_bias,
    w_query,
    q_bias,
    w_key,
    w_value,
    v_bias,
    w_out,
    out_bias,
    ln2_gain,
    ln2_bias,
    w_fc1,
    fc1_bias,
    w_fc2,
    fc2_bias,
):
    ORDER.clear()
    row_block, quarter, width = activations.shape
    assert row_block == 2
    shard = w_query.shape[1]
    heads = shard // HEAD_DIM
    padded = -(-shard // LANES) * LANES
    half = 2 * quarter
    group = lax.axis_index("group")
    core_index = group % 2
    core = core_index.astype(jnp.int32).reshape(1)

    small = jnp.concatenate(
        [ln1_gain, ln1_bias, out_bias, ln2_gain, ln2_bias, fc2_bias, q_bias, v_bias, fc1_bias]
    ).reshape(-1, shard)
    position = jnp.stack([core_index, group]).astype(jnp.int32)
    to_chip, to_diagonal, to_core, mine = split_inputs(
        activations, small, position, shard, padded
    )
    from_chip, from_diagonal = chip_swap(to_chip), diagonal_swap(to_diagonal)
    core_piece = core_swap(to_core)

    packed = pack_attention(w_query, w_key, w_value, w_out)
    w_att = packed, core_swap(packed)
    own_ids = lax.dynamic_slice_in_dim(picture_ids, group * quarter, quarter, 1)[..., None]
    grad_to_chip, grad_to_diagonal, grad_own, grad_to_core = split_grads(out_grad, own_ids, core)
    grad_core = core_swap(grad_to_core)
    grad_far = chip_swap(grad_to_chip), diagonal_swap(grad_to_diagonal)
    grad_near = grad_to_chip, grad_core
    up_own, down_own = pack_mlp(w_fc1, w_fc2)
    up_core, down_core = core_swap(up_own), core_swap(down_own)

    row_ids = lax.dynamic_index_in_dim(picture_ids, core_index, 0, keepdims=False)
    row_ids = row_ids.reshape(4, quarter)
    ids = jnp.concatenate(
        [lax.dynamic_index_in_dim(row_ids, group ^ i, 0, keepdims=False) for i in range(4)]
    )
    lane = jnp.arange(2 * LANES)
    same = ids[:, None] == (lane % HEAD_DIM - 1)[None, :]
    marks = jnp.where(
        lane[None, :] < LANES, jnp.where(same, 0.0, 1.0), jnp.where(same, MASKED, 0.0)
    ).astype(BF)

    normed_one, hat_one, sides, out_w, vectors, bias = project(
        activations, mine, (core_piece, from_chip, from_diagonal), w_att, padded, core
    )
    att_1, inv_1, exp_1, branch_1 = attend(sides, marks, out_w, 1, heads, BF)
    branch_received = chip_swap(branch_1)
    att_0, inv_0, exp_0, branch_0 = attend(sides, after(marks, *grad_far), out_w, 0, heads, F32)
    ups, downs = stack_weights((up_own, down_own), (up_core, down_core))
    middle, normed_own = second_norm(
        activations, core_piece, branch_0, branch_received, vectors, core
    )
    normed_two = normed_own, chip_swap(normed_own)

    activated, hidden, mlp_0, back_0, up_sum_0 = mlp(
        normed_two[0], grad_near, ups, downs, bias, 0, F32, ()
    )
    activated, hidden, mlp_1, back_1, up_sum_1 = mlp(
        normed_two[1], grad_far, ups, downs, bias, 1, BF, (activated, hidden)
    )
    grad_received = chip_swap(back_1)

    state = {}

    def advance(name):
        pending = state[name]
        if pending.rows is None and pending.at < len(pending.groups):
            pending.scatter()
        elif pending.rows is None:
            pending.total(state["small"] if name == "a" else None)
            pending.collect()
        elif pending.at > 0:
            pending.combine()
            pending.collect()

    def attention_grads(side):
        return attention_weight_grad(
            (att_0, att_1),
            state["branch"],
            (state["dq_0"][side], state["dq_1"][side]),
            state["dk"][side],
            state["dv"][side],
            normed_one,
            shard,
            side,
        )

    def first_grad(half_index, dtype):
        return input_grad(
            state[f"dq_{half_index}"], state["dk"], state["dv"], w_att, hat_one, half_index, dtype
        )

    for token in SEQUENCE:
        if token == "W1":
            state["sent"] = core_swap(mlp_weight_grad(normed_two, grad_near + grad_far, activated, hidden, 1))
        elif token == "R":
            state["out"] = chip_swap(after(mlp_1, ORDER[0]))
        elif token == "W0":
            kept = mlp_weight_grad(normed_two, grad_near + grad_far, activated, hidden, 0)
            state["m"] = ReplicaSum(kept, state["sent"], replicas, *MLP_GROUPS)
        elif token == "N":
            grad_middle, branch_own, late_sums = second_norm_back(
                middle, back_0, grad_received, grad_own, grad_core, vectors
            )
            state["branch"] = branch_own, chip_swap(branch_own)
        elif token == "B0":
            dq, dk_0, dv_0 = attend_back(
                state["branch"][0], out_w, att_0, inv_0, exp_0, sides, 0, heads, None
            )
            state["dq_0"] = dq[0], dq[1]
        elif token == "B1":
            dq, dk, dv = attend_back(
                state["branch"][1], out_w, att_1, inv_1, exp_1, sides, 1, heads, (dk_0, dv_0)
            )
            state["dq_1"], state["dk"], state["dv"] = [(a[0], a[1]) for a in (dq, dk, dv)]
        elif token in ("B11", "B10"):
            side = int(token[2])
            parts = attend_back(
                state["branch"][1], out_w, att_1, inv_1, exp_1, sides, 1, heads, (dk_0, dv_0), side
            )
            for key, part in zip(("dq_1", "dk", "dv"), parts):
                state.setdefault(key, {})[side] = part[0]
        elif token == "A1":
            state["sent"] = core_swap(attention_grads(1))
        elif token == "A0":
            state["a"] = ReplicaSum(attention_grads(0), state["sent"], replicas, *ATT_GROUPS)
        elif token == "I1":
            for key in ("dq_1", "dk", "dv"):
                state[key] = state[key][0], state[key][1]
            first_1, norm_1 = first_grad(1, BF)
            if RS4_EARLY:
                first_received = chip_swap(first_1)
        elif token == "I0":
            first_0, norm_0 = first_grad(0, F32)
        elif token == "G":
            wide, bias_sums = small_grads(
                norm_0, norm_1, late_sums, (*state["dq_0"], *state["dq_1"]), state["dv"],
                up_sum_0, up_sum_1,
            )
            wide_received = chip_swap(wide)
            if not RS4_EARLY:
                first_received = chip_swap(after(first_1, wide))
        elif token == "F":
            output_home, output_sent = finish_output(middle, mlp_0, state["out"], vectors, core)
            output_received = core_swap(output_sent)
        elif token == "C":
            small_own, small_sent = small_chip(wide, wide_received, bias_sums)
            small_core = core_swap(small_sent)
        elif token == "U":
            state["small"] = small_sum(small_own, small_core)
        elif token == "L":
            input_home, input_sent = first_norm_back(
                activations, core_piece, grad_middle, first_0, first_received, vectors, core
            )
            input_received = core_swap(input_sent)
        else:
            advance(token)
    for name in ("m", "a"):
        while state[name].rows is None or state[name].at > 0:
            advance(name)
    state["m"].combine(join_mlp)
    state["a"].combine(lambda parts, mine: join_weights(parts, mine, shard, 8))
    weights, small = state["a"].rows[:4], state["a"].rows[4]
    mlp_sum = state["m"]

    def place(home, received):
        return lax.dynamic_update_slice(home, received[None], (1 - core_index, 0, 0))

    mine = lax.dynamic_slice_in_dim(small[:6], group * shard, shard, 1)

    return (
        place(output_home, output_received),
        place(input_home, input_received),
        mine[0],
        mine[1],
        weights[1].T,
        small[6, :shard],
        weights[2].T,
        weights[3].T,
        small[6, padded : padded + shard],
        weights[0],
        mine[4],
        mine[2],
        mine[3],
        mlp_sum.rows[0],
        small[7],
        mlp_sum.rows[1],
        mine[5],
    )


def solution(mesh):
    replicas = mesh.shape["replica"]
    assert mesh.shape["group"] == 4
    patches = P("replica", "group", None)
    vector = P("group")
    columns = P(None, "group")
    rows = P("group", None)
    parameters = (vector, vector, columns, vector, columns, columns, vector, rows)
    parameters += (vector, vector, vector, columns, vector, rows, vector)

    def program(*arguments):
        return per_device(replicas, *arguments)

    return jax.shard_map(
        program,
        mesh=mesh,
        in_specs=(patches, patches, P("replica", None)) + parameters,
        out_specs=(patches, patches) + parameters,
        check_vma=False,
    )
```

profile of v0, /device:TPU:0, one launch (start us, length us, event | category | flops | bytes accessed | tf_op | source)
XLA Modules:
  0.0 275.6 jit_solution(13634616373232651470)
XLA Ops:
  23.5 6.0 %collective-permute-done.2.fourth = bf16[272,768]{1,0:T(8,128)(2,1)} collective-permute-done((bf16[272,768]{1,0:T(8,128)(2,1)}, bf16[272,768]{1,0:T(8,128)(2,1)}, u32[]{:S(2)}, u32[]{:S(2)}) %collective-permute-start.2) | collective-permute-done | bytes 417824 | tf_op jit(solution)/shard_map/ppermute | solution.py:809
  31.4 6.4 %project.1 = (bf16[1024,768]{1,0:T(8,128)(2,1)}, bf16[1024,768]{1,0:T(8,128)(2,1)}, bf16[2,1024,768]{2,1,0:T(8,128)(2,1)S(1)}, bf16[2,256,768]{2,1,0:T(8,128)(2,...) custom-call(s32[1]{0:T(128)} %bitcast.core_ref, f32[2,256,768]{2,1,0:T(8,128)} %own.5, ...), custom_call_target="tpu_custom_call" | custom-call | flops 8000000000 | bytes 1 | tf_op jit(solution)/shard_map/project/pallas_call | solution.py:97
  37.8 8.0 %attend_1.1 = (bf16[2,512,256]{2,1,0:T(8,128)(2,1)}, f32[2,512,256]{2,1,0:T(8,128)}, bf16[6,512,1024]{2,1,0:T(8,128)(2,1)}, bf16[512,768]{1,0:T(8,128)(2,1)S(1)}) custom-call(bf16[2,1024,768]{2,1,0:T(8,128)(2,1)S(1)} %get-tuple-element.141.sides, bf16[1024,256]{1,0:T(8,128)(2,1)S(1)} %fusion.1.marks, bf16[2,256,768]{2,1,0:T(8,128)(2,1)S(1)} %get-tuple-element.146.w_ref), custom_call_target="tpu_custom_call" | custom-call | flops 8000000000 | bytes 1 | tf_op jit(solution)/shard_map/attend_1/pallas_call | solution.py:97
  46.4 8.0 %attend_0.1 = (bf16[2,512,256]{2,1,0:T(8,128)(2,1)}, f32[2,512,256]{2,1,0:T(8,128)}, bf16[6,512,1024]{2,1,0:T(8,128)(2,1)}, f32[512,768]{1,0:T(8,128)S(1)}) custom-call(bf16[2,1024,768]{2,1,0:T(8,128)(2,1)S(1)} %get-tuple-element.141.sides, bf16[1024,256]{1,0:T(8,128)(2,1)S(1)} %fusion.1.marks, bf16[2,256,768]{2,1,0:T(8,128)(2,1)S(1)} %get-tuple-element.146.w_ref), custom_call_target="tpu_custom_call" | custom-call | flops 8000000000 | bytes 1 | tf_op jit(solution)/shard_map/attend_0/pallas_call | solution.py:97
  54.7 11.0 %collective-permute-done.6.recv_ref = bf16[512,768]{1,0:T(8,128)(2,1)S(1)} collective-permute-done((bf16[512,768]{1,0:T(8,128)(2,1)S(1)}, bf16[512,768]{1,0:T(8,128)(2,1)S(1)}, u32[]{:S(2)}, u32[]{:S(2)}) %collective-permute-start.6) | collective-permute-done | bytes 786464 | tf_op jit(solution)/shard_map/ppermute | solution.py:809
  69.4 9.3 %mlp_0.1 = (bf16[2,1024,768]{2,1,0:T(8,128)(2,1)S(1)}, bf16[2,1024,768]{2,1,0:T(8,128)(2,1)S(1)}, f32[512,768]{1,0:T(8,128)}, f32[512,768]{1,0:T(8,128)}, f32[2,1,768]{2,1,0:T(1,128)S(1)}) custom-call(bf16[512,768]{1,0:T(8,128)(2,1)S(1)} %get-tuple-element.158.n_ref.n_0, bf16[256,768]{1,0:T(8,128)(2,1)} %get-tuple-element.173.g_0, ...), custom_call_target="tpu_custom_call" | custom-call | flops 8000000000 | bytes 1 | tf_op jit(solution)/shard_map/mlp_0/pallas_call | solution.py:97
  78.6 9.6 %collective-permute-done.10.n_ref.n_1 = bf16[512,768]{1,0:T(8,128)(2,1)S(1)} collective-permute-done((bf16[512,768]{1,0:T(8,128)(2,1)S(1)}, bf16[512,768]{1,0:T(8,128)(2,1)S(1)}, u32[]{:S(2)}, u32[]{:S(2)}) %collective-permute-start.10) | collective-permute-done | bytes 786464 | tf_op jit(solution)/shard_map/ppermute | solution.py:809
  88.2 8.1 %mlp_1.1 = (bf16[2,1024,768]{2,1,0:T(8,128)(2,1)S(1)}, bf16[2,1024,768]{2,1,0:T(8,128)(2,1)S(1)}, bf16[512,768]{1,0:T(8,128)(2,1)S(1)}, bf16[512,768]{1,0:T(8,128)(2,1)S(1)}, f32[2,1,768]{2,1,0:T(1,128)S(1)}) custom-call(bf16[512,768]{1,0:T(8,128)(2,1)S(1)} %collective-permute-done.10.n_ref.n_1, ...), custom_call_target="tpu_custom_call", output_to_operand_aliasing={{0}: (6, {}), {1}: (7, {})} | custom-call | flops 8000000000 | bytes 1 | tf_op jit(solution)/shard_map/mlp_1/pallas_call | solution.py:97
  97.3 5.8 %mlp_sent.1 = bf16[1536,768]{1,0:T(8,128)(2,1)} custom-call(bf16[512,768]{1,0:T(8,128)(2,1)S(1)} %get-tuple-element.158.n_ref.n_0, bf16[512,768]{1,0:T(8,128)(2,1)S(1)} %collective-permute-done.10.n_ref.n_1, bf16[256,768]{1,0:T(8,128)(2,1)} %get-tuple-element.173.g_0, f32[256,768]{1,0:T(8,128)S(1)} %collective-permute-done.9.g_1.partner, ...), custom_call_target="tpu_custom_call" | custom-call | flops 1 | bytes 1 | tf_op jit(solution)/shard_map/mlp_sent/pallas_call | solution.py:97
  111.7 3.8 %mlp_kept.1.kept_ref = bf16[1536,768]{1,0:T(8,128)(2,1)S(1)} custom-call(bf16[512,768]{1,0:T(8,128)(2,1)S(1)} %copy-done.18, bf16[512,768]{1,0:T(8,128)(2,1)S(1)} %copy-done.20, bf16[256,768]{1,0:T(8,128)(2,1)} %get-tuple-element.173.g_0, f32[256,768]{1,0:T(8,128)S(1)} %copy-done.9, bf16[256,768]{1,0:T(8,128)(2,1)} %collective-permute-done.4.g_0.g_2, ...), custom_call_target="tpu_custom_call" | custom-call | flops 6000000000 | bytes 1 | tf_op jit(solution)/shard_map/mlp_kept/pallas_call | solution.py:97
  124.5 5.4 %second_norm_back.1 = (f32[512,768]{1,0:T(8,128)}, bf16[512,768]{1,0:T(8,128)(2,1)S(1)}, f32[4,768]{1,0:T(4,128)S(1)}) custom-call(f32[512,768]{1,0:T(8,128)} %get-tuple-element.157.middle_ref, f32[512,768]{1,0:T(8,128)} %get-tuple-element.176.grad_ref, bf16[512,768]{1,0:T(8,128)(2,1)} %collective-permute-done.14.recv_ref, ...), custom_call_target="tpu_custom_call" | custom-call | flops 1 | bytes 1 | tf_op jit(solution)/shard_map/second_norm_back/pallas_call | solution.py:97
  130.2 11.5 %attend_back_0.1 = (bf16[2,512,256]{2,1,0:T(8,128)(2,1)S(1)}, f32[2,1024,256]{2,1,0:T(8,128)S(1)}, f32[2,1024,256]{2,1,0:T(8,128)S(1)}) custom-call(bf16[512,768]{1,0:T(8,128)(2,1)S(1)} %get-tuple-element.182.grad_ref.g_0, bf16[2,256,768]{2,1,0:T(8,128)(2,1)S(1)} %copy-done.16, bf16[2,512,256]{2,1,0:T(8,128)(2,1)} %get-tuple-element.152.at_ref.at_0, ...), custom_call_target="tpu_custom_call" | custom-call | flops 6000000000 | bytes 1 | tf_op jit(solution)/shard_map/attend_back_0/pallas_call | solution.py:97
  141.7 5.7 %collective-permute-done.13.refs_0_ = bf16[768,768]{1,0:T(8,128)(2,1)} collective-permute-done((bf16[768,768]{1,0:T(8,128)(2,1)}, bf16[768,768]{1,0:T(8,128)(2,1)}, u32[]{:S(2)}, u32[]{:S(2)}) %collective-permute-start.13) | collective-permute-done | bytes 1179680 | tf_op jit(solution)/shard_map/ppermute | solution.py:809
  151.9 11.9 %attend_back_1.1 = (bf16[2,512,256]{2,1,0:T(8,128)(2,1)S(1)}, bf16[2,1024,256]{2,1,0:T(8,128)(2,1)S(1)}, bf16[2,1024,256]{2,1,0:T(8,128)(2,1)S(1)}) custom-call(bf16[512,768]{1,0:T(8,128)(2,1)S(1)} %collective-permute-done.16.grad_ref.g_1, bf16[2,256,768]{2,1,0:T(8,128)(2,1)S(1)} %copy-done.16, bf16[2,512,256]{2,1,0:T(8,128)(2,1)} %get-tuple-element.147.at_ref.at_1, ...), custom_call_target="tpu_custom_call" | custom-call | flops 1 | bytes 1 | tf_op jit(solution)/shard_map/attend_back_1/pallas_call | solution.py:97
  178.8 8.0 %collective-permute-done.17.refs_0_ = bf16[192,768]{1,0:T(8,128)(2,1)S(1)} collective-permute-done((bf16[192,768]{1,0:T(8,128)(2,1)S(1)}, bf16[192,768]{1,0:T(8,128)(2,1)S(1)}, u32[]{:S(2)}, u32[]{:S(2)}) %collective-permute-start.17) | collective-permute-done | bytes 294944 | tf_op jit(solution)/shard_map/ppermute | solution.py:809
  193.7 3.7 %input_grad_0.1 = (f32[512,768]{1,0:T(8,128)}, f32[2,768]{1,0:T(2,128)S(1)}) custom-call(bf16[512,256]{1,0:T(8,128)(2,1)S(1)} %get-tuple-element.208.q_0.rest_0_, bf16[512,256]{1,0:T(8,128)(2,1)S(1)} %get-tuple-element.198.q_0.q_1.rest_1_, bf16[1024,256]{1,0:T(8,128)(2,1)S(1)} %get-tuple-element.266.k_ref.k_0, ...), custom_call_target="tpu_custom_call" | custom-call | flops 1 | bytes 1 | tf_op jit(solution)/shard_map/input_grad_0/pallas_call | solution.py:97
  197.7 6.1 %collective-permute-done.19.refs_1_ = bf16[192,768]{1,0:T(8,128)(2,1)S(1)} collective-permute-done((bf16[192,768]{1,0:T(8,128)(2,1)S(1)}, bf16[192,768]{1,0:T(8,128)(2,1)S(1)}, u32[]{:S(2)}, u32[]{:S(2)}) %collective-permute-start.19) | collective-permute-done | bytes 294944 | tf_op jit(solution)/shard_map/ppermute | solution.py:809
  214.4 4.1 %collective-permute-start.25 = (bf16[192,768]{1,0:T(8,128)(2,1)S(1)}, bf16[192,768]{1,0:T(8,128)(2,1)S(1)}, u32[]{:S(2)}, u32[]{:S(2)}) collective-permute-start(bf16[192,768]{1,0:T(8,128)(2,1)S(1)} %get-tuple-element.225), channel_id=1, source_target_pairs={{0,2},{1,3},{2,0},{3,1},{4,6},{5,7},{6,4},{7,5},{8,10},{9,11},{10,... | collective-permute-start | bytes 884744 | tf_op jit(solution)/shard_map/ppermute | solution.py:809
  218.6 7.2 %collective-permute-done.25.refs_0_ = bf16[192,768]{1,0:T(8,128)(2,1)S(1)} collective-permute-done((bf16[192,768]{1,0:T(8,128)(2,1)S(1)}, bf16[192,768]{1,0:T(8,128)(2,1)S(1)}, u32[]{:S(2)}, u32[]{:S(2)}) %collective-permute-start.25) | collective-permute-done | bytes 294944 | tf_op jit(solution)/shard_map/ppermute | solution.py:809
  228.6 4.3 %first_norm_back.1 = (f32[2,256,768]{2,1,0:T(8,128)}, f32[256,768]{1,0:T(8,128)}) custom-call(s32[1]{0:T(128)} %bitcast.core_ref, f32[2,256,768]{2,1,0:T(8,128)} %own.5, f32[272,768]{1,0:T(8,128)} %collective-permute-done.second.core_piece, f32[512,768]{1,0:T(8,128)} %get-tuple-element.215.middle_ref, f32[512,768]{1,0:T(8,128)} %get-tuple-element.216.grad_ref, ...), custom_call_target="tpu_custom_call" | custom-call | flops 1 | bytes 1 | tf_op jit(solution)/shard_map/first_norm_back/pallas_call | solution.py:97
  233.0 4.0 %collective-permute-done.28.refs_0_ = bf16[96,768]{1,0:T(8,128)(2,1)S(1)} collective-permute-done((bf16[96,768]{1,0:T(8,128)(2,1)S(1)}, bf16[96,768]{1,0:T(8,128)(2,1)S(1)}, u32[]{:S(2)}, u32[]{:S(2)}) %collective-permute-start.28) | collective-permute-done | bytes 147488 | tf_op jit(solution)/shard_map/ppermute | solution.py:809
  238.1 8.8 %collective-permute-done.29.refs_1_ = bf16[104,768]{1,0:T(8,128)(2,1)S(1)} collective-permute-done((bf16[104,768]{1,0:T(8,128)(2,1)S(1)}, bf16[104,768]{1,0:T(8,128)(2,1)S(1)}, u32[]{:S(2)}, u32[]{:S(2)}) %collective-permute-start.29) | collective-permute-done | bytes 159776 | tf_op jit(solution)/shard_map/ppermute | solution.py:809
  247.0 9.2 %collective-permute-done.30.refs_1_ = bf16[200,768]{1,0:T(8,128)(2,1)S(1)} collective-permute-done((bf16[200,768]{1,0:T(8,128)(2,1)S(1)}, bf16[200,768]{1,0:T(8,128)(2,1)S(1)}, u32[]{:S(2)}, u32[]{:S(2)}) %collective-permute-start.30) | collective-permute-done | bytes 307232 | tf_op jit(solution)/shard_map/ppermute | solution.py:809
  263.3 7.8 %collective-permute-done.32.refs_1_ = bf16[392,768]{1,0:T(8,128)(2,1)} collective-permute-done((bf16[392,768]{1,0:T(8,128)(2,1)S(1)}, bf16[392,768]{1,0:T(8,128)(2,1)}, u32[]{:S(2)}, u32[]{:S(2)}) %collective-permute-start.32) | collective-permute-done | bytes 602144 | tf_op jit(solution)/shard_map/ppermute | solution.py:809
  (164 shorter events, 100.9 us)
Async XLA Ops:
  6.6 24.7 %collective-permute-start.3 = (bf16[1024,768]{1,0:T(8,128)(2,1)S(1)}, bf16[1024,768]{1,0:T(8,128)(2,1)S(1)}, u32[]{:S(2)}, u32[]{:S(2)}) collective-permute-start(bf16[1024,768]{1,0:T(8,128)(2,1)S(1)} %pack_attention.1.w_0), channel_id=1, source_target_pairs={{0,8},{8,0},{16,24},{24,16},{1,9},{9,1},{17,25},{25,17},{2,10},{10... | collective-permute-start | bytes 4718600 | tf_op jit(solution)/shard_map/ppermute | solution.py:809
  7.2 24.2 %collective-permute-start = (f32[272,768]{1,0:T(8,128)}, f32[272,768]{1,0:T(8,128)}, u32[]{:S(2)}, u32[]{:S(2)}) collective-permute-start(f32[272,768]{1,0:T(8,128)} %get-tuple-element.131), channel_id=1, source_target_pairs={{0,8},{8,0},{16,24},{24,16},{1,9},{9,1},{17,25},{25,17},{2,10},{10... | collective-permute-start | bytes 2506760 | tf_op jit(solution)/shard_map/ppermute | solution.py:809
  7.2 15.7 %collective-permute-start.1 = (bf16[272,768]{1,0:T(8,128)(2,1)}, bf16[272,768]{1,0:T(8,128)(2,1)}, u32[]{:S(2)}, u32[]{:S(2)}) collective-permute-start(bf16[272,768]{1,0:T(8,128)(2,1)} %get-tuple-element.139), channel_id=1, source_target_pairs={{0,16},{8,24},{16,0},{24,8},{1,17},{9,25},{17,1},{25,9},{2,18},{10... | collective-permute-start | bytes 1253384 | tf_op jit(solution)/shard_map/ppermute | solution.py:809
  10.1 19.3 %collective-permute-start.2 = (bf16[272,768]{1,0:T(8,128)(2,1)}, bf16[272,768]{1,0:T(8,128)(2,1)}, u32[]{:S(2)}, u32[]{:S(2)}) collective-permute-start(bf16[272,768]{1,0:T(8,128)(2,1)} %get-tuple-element.140), channel_id=1, source_target_pairs={{0,24},{8,16},{16,8},{24,0},{1,25},{9,17},{17,9},{25,1},{2,26},{10... | collective-permute-start | bytes 1253384 | tf_op jit(solution)/shard_map/ppermute | solution.py:809
  16.1 30.0 %collective-permute-start.4 = (bf16[256,768]{1,0:T(8,128)(2,1)}, bf16[256,768]{1,0:T(8,128)(2,1)}, u32[]{:S(2)}, u32[]{:S(2)}) collective-permute-start(bf16[256,768]{1,0:T(8,128)(2,1)} %get-tuple-element.173.g_0), channel_id=1, source_target_pairs={{0,16},{8,24},{16,0},{24,8},{1,17},{9,25},{17,1},{25,9},{2,18},{10... | collective-permute-start | bytes 1179656 | tf_op jit(solution)/shard_map/ppermute | solution.py:809
  23.0 31.4 %collective-permute-start.7 = (bf16[768,768]{1,0:T(8,128)(2,1)}, bf16[768,768]{1,0:T(8,128)(2,1)S(1)}, u32[]{:S(2)}, u32[]{:S(2)}) collective-permute-start(bf16[768,768]{1,0:T(8,128)(2,1)} %copy-done.11), channel_id=1, source_target_pairs={{0,8},{8,0},{16,24},{24,16},{1,9},{9,1},{17,25},{25,17},{2,10},{10... | collective-permute-start | bytes 3538952 | tf_op jit(solution)/shard_map/ppermute | solution.py:809
  29.4 16.9 %collective-permute-start.5 = (bf16[256,768]{1,0:T(8,128)(2,1)}, bf16[256,768]{1,0:T(8,128)(2,1)S(1)}, u32[]{:S(2)}, u32[]{:S(2)}) collective-permute-start(bf16[256,768]{1,0:T(8,128)(2,1)} %copy-done.28), channel_id=1, source_target_pairs={{0,24},{8,16},{16,8},{24,0},{1,25},{9,17},{17,9},{25,1},{2,26},{10... | collective-permute-start | bytes 1179656 | tf_op jit(solution)/shard_map/ppermute | solution.py:809
  31.3 23.0 %collective-permute-start.8 = (bf16[768,768]{1,0:T(8,128)(2,1)}, bf16[768,768]{1,0:T(8,128)(2,1)S(1)}, u32[]{:S(2)}, u32[]{:S(2)}) collective-permute-start(bf16[768,768]{1,0:T(8,128)(2,1)} %copy-done.13), channel_id=1, source_target_pairs={{0,8},{8,0},{16,24},{24,16},{1,9},{9,1},{17,25},{25,17},{2,10},{10... | collective-permute-start | bytes 3538952 | tf_op jit(solution)/shard_map/ppermute | solution.py:809
  45.8 19.9 %collective-permute-start.6 = (bf16[512,768]{1,0:T(8,128)(2,1)S(1)}, bf16[512,768]{1,0:T(8,128)(2,1)S(1)}, u32[]{:S(2)}, u32[]{:S(2)}) collective-permute-start(bf16[512,768]{1,0:T(8,128)(2,1)S(1)} %get-tuple-element.150), channel_id=1, source_target_pairs={{0,16},{8,24},{16,0},{24,8},{1,17},{9,25},{17,1},{25,9},{2,18},{10... | collective-permute-start | bytes 2359304 | tf_op jit(solution)/shard_map/ppermute | solution.py:809
  46.1 23.2 %collective-permute-start.9 = (f32[256,768]{1,0:T(8,128)S(1)}, f32[256,768]{1,0:T(8,128)S(1)}, u32[]{:S(2)}, u32[]{:S(2)}) collective-permute-start(f32[256,768]{1,0:T(8,128)S(1)} %copy-done.26), channel_id=1, source_target_pairs={{0,8},{8,0},{16,24},{24,16},{1,9},{9,1},{17,25},{25,17},{2,10},{10... | collective-permute-start | bytes 2359304 | tf_op jit(solution)/shard_map/ppermute | solution.py:809
  69.1 19.1 %collective-permute-start.10 = (bf16[512,768]{1,0:T(8,128)(2,1)S(1)}, bf16[512,768]{1,0:T(8,128)(2,1)S(1)}, u32[]{:S(2)}, u32[]{:S(2)}) collective-permute-start(bf16[512,768]{1,0:T(8,128)(2,1)S(1)} %get-tuple-element.158.n_ref.n_0), channel_id=1, source_target_pairs={{0,16},{8,24},{16,0},{24,8},{1,17},{9,25},{17,1},{25,9},{2,18},{10... | collective-permute-start | bytes 2359304 | tf_op jit(solution)/shard_map/ppermute | solution.py:809
  103.1 20.3 %collective-permute-start.14 = (bf16[512,768]{1,0:T(8,128)(2,1)}, bf16[512,768]{1,0:T(8,128)(2,1)}, u32[]{:S(2)}, u32[]{:S(2)}) collective-permute-start(bf16[512,768]{1,0:T(8,128)(2,1)} %copy-done.27), channel_id=1, source_target_pairs={{0,16},{8,24},{16,0},{24,8},{1,17},{9,25},{17,1},{25,9},{2,18},{10... | collective-permute-start | bytes 2359304 | tf_op jit(solution)/shard_map/ppermute | solution.py:809
  119.0 28.4 %collective-permute-start.13 = (bf16[768,768]{1,0:T(8,128)(2,1)}, bf16[768,768]{1,0:T(8,128)(2,1)}, u32[]{:S(2)}, u32[]{:S(2)}) collective-permute-start(bf16[768,768]{1,0:T(8,128)(2,1)} %get-tuple-element.175), channel_id=1, source_target_pairs={{0,1},{1,0},{2,3},{3,2},{4,5},{5,4},{6,7},{7,6},{8,9},{9,8},{10,11... | collective-permute-start | bytes 3538952 | tf_op jit(solution)/shard_map/ppermute | solution.py:809
  129.9 22.0 %collective-permute-start.16 = (bf16[512,768]{1,0:T(8,128)(2,1)S(1)}, bf16[512,768]{1,0:T(8,128)(2,1)S(1)}, u32[]{:S(2)}, u32[]{:S(2)}) collective-permute-start(bf16[512,768]{1,0:T(8,128)(2,1)S(1)} %get-tuple-element.182.grad_ref.g_0), channel_id=1, source_target_pairs={{0,16},{8,24},{16,0},{24,8},{1,17},{9,25},{17,1},{25,9},{2,18},{10... | collective-permute-start | bytes 2359304 | tf_op jit(solution)/shard_map/ppermute | solution.py:809
  170.0 16.8 %collective-permute-start.17 = (bf16[192,768]{1,0:T(8,128)(2,1)S(1)}, bf16[192,768]{1,0:T(8,128)(2,1)S(1)}, u32[]{:S(2)}, u32[]{:S(2)}) collective-permute-start(bf16[192,768]{1,0:T(8,128)(2,1)S(1)} %get-tuple-element.197), channel_id=1, source_target_pairs={{0,4},{1,5},{2,6},{3,7},{4,0},{5,1},{6,2},{7,3},{8,12},{9,13},{10,... | collective-permute-start | bytes 884744 | tf_op jit(solution)/shard_map/ppermute | solution.py:809
  172.9 32.6 %collective-permute-start.11 = (bf16[512,768]{1,0:T(8,128)(2,1)S(1)}, bf16[512,768]{1,0:T(8,128)(2,1)S(1)}, u32[]{:S(2)}, u32[]{:S(2)}) collective-permute-start(bf16[512,768]{1,0:T(8,128)(2,1)S(1)} %copy-done.24), channel_id=1, source_target_pairs={{0,16},{8,24},{16,0},{24,8},{1,17},{9,25},{17,1},{25,9},{2,18},{10... | collective-permute-start | bytes 2359304 | tf_op jit(solution)/shard_map/ppermute | solution.py:809
  187.8 16.0 %collective-permute-start.19 = (bf16[192,768]{1,0:T(8,128)(2,1)S(1)}, bf16[192,768]{1,0:T(8,128)(2,1)S(1)}, u32[]{:S(2)}, u32[]{:S(2)}) collective-permute-start(bf16[192,768]{1,0:T(8,128)(2,1)S(1)} %add_all.2.refs_0_), channel_id=1, source_target_pairs={{0,4},{1,5},{2,6},{3,7},{4,0},{5,1},{6,2},{7,3},{8,12},{9,13},{10,... | collective-permute-start | bytes 884744 | tf_op jit(solution)/shard_map/ppermute | solution.py:809
  187.9 24.6 %collective-permute-start.22 = (bf16[384,768]{1,0:T(8,128)(2,1)S(1)}, bf16[384,768]{1,0:T(8,128)(2,1)S(1)}, u32[]{:S(2)}, u32[]{:S(2)}) collective-permute-start(bf16[384,768]{1,0:T(8,128)(2,1)S(1)} %get-tuple-element.218), channel_id=1, source_target_pairs={{0,1},{1,0},{2,3},{3,2},{4,5},{5,4},{6,7},{7,6},{8,9},{9,8},{10,11... | collective-permute-start | bytes 1769480 | tf_op jit(solution)/shard_map/ppermute | solution.py:809
  192.1 36.5 %collective-permute-start.21 = (bf16[512,768]{1,0:T(8,128)(2,1)S(1)}, bf16[512,768]{1,0:T(8,128)(2,1)S(1)}, u32[]{:S(2)}, u32[]{:S(2)}) collective-permute-start(bf16[512,768]{1,0:T(8,128)(2,1)S(1)} %get-tuple-element.217), channel_id=1, source_target_pairs={{0,16},{8,24},{16,0},{24,8},{1,17},{9,25},{17,1},{25,9},{2,18},{10... | collective-permute-start | bytes 2359304 | tf_op jit(solution)/shard_map/ppermute | solution.py:809
  203.9 14.7 %collective-permute-start.26 = (bf16[384,768]{1,0:T(8,128)(2,1)S(1)}, bf16[384,768]{1,0:T(8,128)(2,1)S(1)}, u32[]{:S(2)}, u32[]{:S(2)}) collective-permute-start(bf16[384,768]{1,0:T(8,128)(2,1)S(1)} %join.4.refs_0_), channel_id=1, source_target_pairs={{0,2},{1,3},{2,0},{3,1},{4,6},{5,7},{6,4},{7,5},{8,10},{9,11},{10,... | collective-permute-start | bytes 1769480 | tf_op jit(solution)/shard_map/ppermute | solution.py:809
  218.5 38.7 %collective-permute-start.20 = (f32[256,768]{1,0:T(8,128)}, f32[256,768]{1,0:T(8,128)}, u32[]{:S(2)}, u32[]{:S(2)}) collective-permute-start(f32[256,768]{1,0:T(8,128)} %get-tuple-element.214), channel_id=1, source_target_pairs={{0,8},{8,0},{16,24},{24,16},{1,9},{9,1},{17,25},{25,17},{2,10},{10... | collective-permute-start | bytes 2359304 | tf_op jit(solution)/shard_map/ppermute | solution.py:809
  227.9 32.7 %collective-permute-start.31 = (bf16[768,768]{1,0:T(8,128)(2,1)S(1)}, bf16[768,768]{1,0:T(8,128)(2,1)S(1)}, u32[]{:S(2)}, u32[]{:S(2)}) collective-permute-start(bf16[768,768]{1,0:T(8,128)(2,1)S(1)} %join.5.first_ref), channel_id=1, source_target_pairs={{0,1},{1,0},{2,3},{3,2},{4,5},{5,4},{6,7},{7,6},{8,9},{9,8},{10,11... | collective-permute-start | bytes 3538952 | tf_op jit(solution)/shard_map/ppermute | solution.py:809
  238.0 21.4 %collective-permute-start.27 = (f32[256,768]{1,0:T(8,128)}, f32[256,768]{1,0:T(8,128)}, u32[]{:S(2)}, u32[]{:S(2)}) collective-permute-start(f32[256,768]{1,0:T(8,128)} %get-tuple-element.231), channel_id=1, source_target_pairs={{0,8},{8,0},{16,24},{24,16},{1,9},{9,1},{17,25},{25,17},{2,10},{10... | collective-permute-start | bytes 2359304 | tf_op jit(solution)/shard_map/ppermute | solution.py:809
  256.2 14.8 %collective-permute-start.32 = (bf16[392,768]{1,0:T(8,128)(2,1)S(1)}, bf16[392,768]{1,0:T(8,128)(2,1)}, u32[]{:S(2)}, u32[]{:S(2)}) collective-permute-start(bf16[392,768]{1,0:T(8,128)(2,1)S(1)} %join.7.refs_0_), channel_id=1, source_target_pairs={{0,1},{1,0},{2,3},{3,2},{4,5},{5,4},{6,7},{7,6},{8,9},{9,8},{10,11... | collective-permute-start | bytes 1806344 | tf_op jit(solution)/shard_map/ppermute | solution.py:809
  (40 other events, 330.3 us)
where the time goes:
time: 277 us; the launch traced here: 276 us
  Pallas kernels  133 us (48%)
  waiting for transfers between devices  90.4 us (33%)
  starting transfers between devices  28.1 us (10%)
  local copies, waits for them, and re-layouts  22.1 us (8%)
    pallas_call x39, Pallas kernels, launch(): pl.pallas_call(body, grid_spec=pltpu.PrefetchScalarGridSpec(num_scalar_pr...  133 us
    ppermute x33, waiting for transfers between devices, swap(): return lax.ppermute(values, axis, [(i, i ^ bit) for i in range(size)])  90.4 us
    ppermute x33, starting transfers between devices, swap(): return lax.ppermute(values, axis, [(i, i ^ bit) for i in range(size)])  28.1 us
    unnamed x62, local copies, waits for them, and re-layouts  14 us
  transfers between devices with their start and end apart: 33, of which 15 were waited for; matrix products, arithmetic and copies ran while one was open for 2% of the time, Pallas kernels for 39%

commit v1 on v0

--- a/solution.py
+++ b/solution.py
@@ -60,9 +60,9 @@
 
 
 SEQUENCE = (
-    "W1", "R", "W0", "m", "N", "B0", "m", "B1", "m", "A1",
-    "A0", "a", "m", "I1", "I0", "G", "m", "F", "C", "U",
-    "a", "m", "a", "L",
+    "W", "m", "R", "N", "B0", "B2", "m", "B3", "A1", "m",
+    "A0", "a", "m", "I1", "I0", "F", "m", "G", "C", "a",
+    "U", "m", "a", "a", "L", "J",
 )
 COSTS = {
     "project": 8000000000,
@@ -70,8 +70,8 @@
     "attend_0": 8000000000,
     "mlp_0": 8000000000,
     "mlp_1": 8000000000,
-    "mlp_kept": 6000000000,
-    "attend_back_0": 6000000000,
+    "attend_back_0": 14000000000,
+    "attend_back_3": 8000000000,
 }
 MLP_GROUPS = (1, 1)
 ATT_GROUPS = (1, 1)
@@ -489,7 +489,7 @@
     size = quarter // 2
 
     def body(
-        middle_ref, grad_ref, recv_ref, own, partner, vec, out_ref, branch_ref, sum_ref, values
+        middle_ref, grad_ref, recv_ref, own, partner, vec, out_ref, first, second, sum_ref, values
     ):
         step = pl.program_id(0)
         here = step_rows(size)
@@ -507,7 +507,12 @@
         out = values[...] + norm_back(incoming * vec[3:4], hat, inverse)
         branch = out.astype(BF)
         out_ref[...] = out
-        branch_ref[here] = branch
+        for i, ref in enumerate((first, second)):
+
+            @pl.when(step // 2 == i)
+            def _():
+                ref[pl.ds(pl.multiple_of((step % 2) * size, size), size)] = branch
+
         sums = jnp.concatenate(
             [
                 column_sum(incoming * hat),
@@ -535,7 +540,8 @@
         + [(grad_own, own_spec), (grad_partner, None), (vectors, None)],
         [
             (shape(dims, F32), by_step(size, width)),
-            (shape(dims, BF), None),
+            (shape((quarter, width), BF), None),
+            (shape((quarter, width), BF), None),
             (shape((4, width), F32), None),
         ],
         grid=(4,),
@@ -543,63 +549,78 @@
     )
 
 
-def mlp_weight_grad(normed, grads, activated, hidden, side):
+def mlp_weight_grads(normed, grads, activated, hidden):
     rows, width = normed[0].shape
     size = hidden.shape[2]
 
-    def body(n_0, n_1, g_0, g_1, g_2, g_3, act_ref, hid_ref, out_ref):
+    def body(n_0, n_1, g_0, g_1, g_2, g_3, act_ref, hid_ref, *outs):
+        kept_ref, sent_refs = outs[0], outs[1:]
+        side = 1 - pl.program_id(0)
         first, second = slice(0, rows), slice(rows, 2 * rows)
         up = dot_tn(n_0[...], hid_ref[side, first]) + dot_tn(n_1[...], hid_ref[side, second])
-        out_ref[:width] = up.astype(BF)
         down, at = None, rows // 2
         for i, ref in enumerate((g_0, g_1, g_2, g_3)):
             part = dot_tn(act_ref[side, i * at : (i + 1) * at], ref[...].astype(BF))
             down = part if down is None else down + part
-        out_ref[width:] = down.astype(BF)
+
+        @pl.when(side == 0)
+        def _():
+            kept_ref[:width] = up.astype(BF)
+            kept_ref[width:] = down.astype(BF)
+
+        @pl.when(side == 1)
+        def _():
+            for i, ref in enumerate(sent_refs):
+                at = (i % 2) * (width // 2)
+                ref[...] = (up, down)[i // 2][at : at + width // 2].astype(BF)
 
     dims = (width + size, width)
-    return launch(
-        body,
-        ("mlp_kept", "mlp_sent")[side],
+    piece = (width // 2, width)
+    return launch(
+        body,
+        "mlp_weight_grads",
         [(a, None) for a in (*normed, *grads, activated, hidden)],
-        [(shape(dims, BF), None)],
-        flops=8 * rows * width * size,
+        [(shape(dims, BF), None)] + [(shape(piece, BF), None)] * 4,
+        grid=(2,),
+        flops=16 * rows * width * size,
         limit=14,
-    )[0]
-
-
-def attend_back(grad, out_w, attended, inverse, exponent, sides, half_index, heads, previous, only=None):
+    )
+
+
+def attend_back(
+    grads, out_w, attended, inverse, exponent, sides, first, block_index, heads, previous, last
+):
     _, length, columns = sides.shape
     padded = columns // 3
-    half, width = grad.shape
-    last = previous is not None
-    steps = half // BLOCK
-
-    def body(grad_ref, w_ref, at_ref, inv_ref, sides, e_ref, *rest):
-        if last:
-            dk_in, dv_in, dq_ref, dk_out, dv_out, dk_sum, dv_sum = rest
-        else:
-            dq_ref, dk_sum, dv_sum = rest
-        step = pl.program_id(0)
-        side = pl.program_id(1) if only is None else only
-        slot = side if only is None else 0
-        here = step_rows()
-        rows = pl.ds(pl.multiple_of(half_index * half + step * BLOCK, BLOCK), BLOCK)
-
-        @pl.when(step == 0)
-        def _():
-            dk_sum[slot] = dk_in[side] if last else jnp.zeros((length, padded), F32)
-            dv_sum[slot] = dv_in[side] if last else jnp.zeros((length, padded), F32)
-
-        first = lane_half()
+    quarter, width = grads[0].shape
+    count = len(grads)
+
+    def body(*refs):
+        grad_refs = refs[:count]
+        w_ref, at_ref, inv_ref, sides, e_ref = refs[count : count + 5]
+        dq_ref, dk_sum, dv_sum, *rounded = refs[count + 5 + len(previous) :]
+        step, side = pl.program_id(0), pl.program_id(1)
+        rows = pl.ds(pl.multiple_of((first + step) * quarter, quarter), quarter)
+
+        if not previous:
+
+            @pl.when(step == 0)
+            def _():
+                dk_sum[side] = jnp.zeros((length, padded), F32)
+                dv_sum[side] = jnp.zeros((length, padded), F32)
+
+        head_lanes = lane_half()
         lane = lax.broadcasted_iota(jnp.int32, (1, LANES), 1)
         zero = jnp.zeros((), BF)
-        grad_att = to_float(dot_nt(grad_ref[here], w_ref[side]).astype(BF))
+        grad_rows = grad_refs[0][...]
+        if count == 2:
+            grad_rows = jnp.where(step == 0, grad_rows, grad_refs[1][...])
+        grad_att = to_float(dot_nt(grad_rows, w_ref[side]).astype(BF))
         scaled = (grad_att * inv_ref[...]).astype(BF)
         product = to_float(scaled) * to_float(at_ref[...])
         dq = [None] * (padded // LANES)
         for head in range(heads):
-            block, lanes = head_place(head, first)
+            block, lanes = head_place(head, head_lanes)
             keys = sides[side, :, padded + block.start : padded + block.stop]
             values = sides[side, :, 2 * padded + block.start : 2 * padded + block.stop]
             grad_head = jnp.where(lanes, scaled[:, block], zero)
@@ -617,56 +638,67 @@
             index = head // 2
             dq[index] = part if dq[index] is None else dq[index] + part
             queries = jnp.where(lanes, sides[side, rows, block], zero)
-            dk_sum[slot, :, block] += dot_tn(grad_scores, queries)
-            dv_sum[slot, :, block] += dot_tn(probs, grad_head)
-        dq_ref[slot, here] = (jnp.concatenate(dq, axis=1) * HEAD_DIM**-0.5).astype(BF)
+            dk_sum[side, :, block] += dot_tn(grad_scores, queries)
+            dv_sum[side, :, block] += dot_tn(probs, grad_head)
+        at = pl.ds(pl.multiple_of(step * quarter, quarter), quarter)
+        dq_ref[side, at] = (jnp.concatenate(dq, axis=1) * HEAD_DIM**-0.5).astype(BF)
 
         if last:
 
-            @pl.when(step == steps - 1)
+            @pl.when(step == count - 1)
             def _():
-                dk_out[slot] = (dk_sum[slot] * HEAD_DIM**-0.5).astype(BF)
-                dv_out[slot] = dv_sum[slot].astype(BF)
-
-    count = 2 if only is None else 1
-    block = pl.BlockSpec((None, BLOCK, padded), lambda i, j: (j if only is None else only, i, 0))
-    ins = [(grad, None), (out_w, None), (attended, block), (inverse, block), (sides, None)]
-    ins += [(exponent, pl.BlockSpec((heads, BLOCK, length), lambda i, j: (j if only is None else only, i, 0)))]
-    if last:
-        ins += [(a, None) for a in previous]
-    sum_dtype = BF if last else F32
-    return launch(
-        body,
-        f"attend_back_{half_index}" + ("" if only is None else f"_{only}"),
+                rounded[0][side] = (dk_sum[side] * HEAD_DIM**-0.5).astype(BF)
+                rounded[1][side] = dv_sum[side].astype(BF)
+
+    block = pl.BlockSpec((None, quarter, padded), lambda i, j: (j, block_index + i, 0))
+    ins = [(a, None) for a in grads]
+    ins += [(out_w, None), (attended, block), (inverse, block), (sides, None)]
+    ins += [
+        (exponent, pl.BlockSpec((heads, quarter, length), lambda i, j: (j, block_index + i, 0)))
+    ]
+    ins += [(a, None) for a in previous]
+    return launch(
+        body,
+        f"attend_back_{first}",
         ins,
-        [(shape((count, half, padded), BF), None)]
-        + [(shape((count, length, padded), sum_dtype), None)] * 2,
-        grid=(steps, count),
-        scratch=[pltpu.VMEM((count, length, padded), F32)] * 2 if last else [],
-        flops=16 * 2 * heads * half * length * 256,
-        limit=20,
+        [(shape((2, count * quarter, padded), BF), None)]
+        + [(shape((2, length, padded), F32), None)] * 2
+        + ([(shape((2, length, padded), BF), None)] * 2 if last else []),
+        grid=(count, 2),
+        aliases={count + 5 + i: 1 + i for i in range(len(previous))},
+        flops=16 * 2 * heads * count * quarter * length * 256,
+        limit=18,
     )
 
 
 def input_grad(queries, keys, values, weights, hat, half_index, dtype):
-    half, padded = queries[0].shape
-    width = hat.shape[1]
-
-    def body(q_0, q_1, k_0, k_1, v_0, v_1, w_0, w_1, hat_ref, out_ref, sum_ref):
-        rows = slice(half_index * half, (half_index + 1) * half)
-        total = None
-        for w_ref, q_ref, k_ref, v_ref in ((w_0, q_0, k_0, v_0), (w_1, q_1, k_1, v_1)):
-            left = jnp.concatenate([q_ref[...], k_ref[rows], v_ref[rows]], axis=1)
-            part = dot_nn(left, w_ref[: 3 * padded])
-            total = part if total is None else total + part
-        out_ref[...] = total.astype(dtype)
-        sums = [column_sum(total * to_float(hat_ref[...])), column_sum(total)]
-        sum_ref[...] = jnp.concatenate(sums, axis=0)
+    half = hat.shape[0] // 2
+    width, padded = hat.shape[1], keys.shape[2]
+    count = len(queries)
+    size = half // count
+
+    def body(*refs):
+        query_refs = refs[:count]
+        k_ref, v_ref, w_0, w_1, hat_ref, out_ref, sum_ref = refs[count:]
+        sums = None
+        for i, q_ref in enumerate(query_refs):
+            at = slice(i * size, (i + 1) * size)
+            rows = slice(half_index * half + i * size, half_index * half + (i + 1) * size)
+            total = None
+            for side, w_ref in enumerate((w_0, w_1)):
+                left = jnp.concatenate([q_ref[side], k_ref[side, rows], v_ref[side, rows]], axis=1)
+                part = dot_nn(left, w_ref[: 3 * padded])
+                total = part if total is None else total + part
+            out_ref[at] = total.astype(dtype)
+            part = [column_sum(total * to_float(hat_ref[at])), column_sum(total)]
+            part = jnp.concatenate(part, axis=0)
+            sums = part if sums is None else sums + part
+        sum_ref[...] = sums
 
     return launch(
         body,
         f"input_grad_{half_index}",
-        [(a, None) for a in (*queries, *keys, *values, *weights)]
+        [(a, None) for a in (*queries, keys, values, *weights)]
         + [(hat, pl.BlockSpec((half, width), lambda i: (half_index, 0)))],
         [
             (shape((half, width), dtype), held(half, width) if dtype == F32 else None),
@@ -677,19 +709,30 @@
 
 
 def attention_weight_grad(attended, grads, queries, keys, values, normed, shard, side):
-    half, padded = queries[0].shape
-    width = normed.shape[1]
-
-    def body(at_0, at_1, g_0, g_1, q_0, q_1, k_ref, v_ref, n_ref, out_ref):
-        n_0, n_1 = n_ref[:half], n_ref[half:]
-        products = [
-            dot_tn(at_0[...], g_0[...]) + dot_tn(at_1[...], g_1[...]),
-            dot_tn(q_0[...], n_0) + dot_tn(q_1[...], n_1),
-            dot_tn(k_ref[...], n_ref[...]),
-            dot_tn(v_ref[...], n_ref[...]),
-        ]
-        for i, part in enumerate(products):
-            out_ref[i * shard : (i + 1) * shard] = part[:shard].astype(BF)
+    length, width = normed.shape
+    padded = keys.shape[2]
+    half, quarter = length // 2, length // 4
+
+    def body(*refs):
+        at_refs, grad_refs, query_refs = refs[:2], refs[2:6], refs[6:9]
+        k_ref, v_ref, n_ref, *outs = refs[9:]
+        out_w = None
+        for i, ref in enumerate(grad_refs):
+            rows = slice((i % 2) * quarter, (i % 2 + 1) * quarter)
+            part = dot_tn(at_refs[i // 2][rows], ref[...])
+            out_w = part if out_w is None else out_w + part
+        query, at = None, 0
+        for ref in query_refs:
+            rows = ref[side]
+            part = dot_tn(rows, n_ref[at : at + rows.shape[0]])
+            query, at = part if query is None else query + part, at + rows.shape[0]
+        key = dot_tn(k_ref[side], n_ref[...])
+        value = dot_tn(v_ref[side], n_ref[...])
+        for i, part in enumerate((out_w, query, key, value)):
+            if side:
+                outs[i][...] = part[:shard].astype(BF)
+            else:
+                outs[0][i * shard : (i + 1) * shard] = part[:shard].astype(BF)
 
     at_spec = pl.BlockSpec((None, half, padded), lambda i: (side, 0, 0))
     dims = (4 * shard, width)
@@ -699,32 +742,39 @@
         [(a, at_spec) for a in attended]
         + [(a, None) for a in (*grads, *queries, keys, values)]
         + [(normed, held(*normed.shape))],
-        [(shape(dims, BF), None)],
-        flops=2 * 2 * half * 4 * padded * width,
+        [(shape((shard, width), BF), None)] * 4 if side else [(shape(dims, BF), None)],
+        flops=2 * length * 4 * padded * width,
         limit=14,
-    )[0]
-
-
-def small_grads(norm_0, norm_1, late, queries, values, up_0, up_1):
-    width = late.shape[1]
-    padded = values[0].shape[1]
-
-    def body(norm_0, norm_1, late, *rest):
-        queries, values, (up_0, up_1, wide_ref, bias_ref) = rest[:4], rest[4:6], rest[6:]
-        wide_ref[...] = jnp.concatenate([norm_0[...] + norm_1[...], late[...]], axis=0).astype(BF)
+    )
+
+
+def small_grads(norms, lates, queries, values, up_sums):
+    width = lates[0].shape[1]
+    padded = values.shape[2]
+    split = len(norms), len(lates), len(queries), 1, len(up_sums)
+
+    def body(*refs):
+        groups, at = [], 0
+        for n in split:
+            groups.append(refs[at : at + n])
+            at += n
+        norms, lates, queries, (v_ref,), ups = groups
+        wide_ref, bias_ref = refs[at:]
+        wide = [sum(ref[...] for ref in norms), sum(ref[...] for ref in lates)]
+        wide_ref[...] = jnp.concatenate(wide, axis=0).astype(BF)
         for side in range(2):
             bias = [
-                column_sum(queries[side][...]) + column_sum(queries[2 + side][...]),
-                column_sum(values[side][...]),
+                sum(column_sum(ref[side]) for ref in queries),
+                column_sum(v_ref[side]),
                 jnp.zeros((1, width - 2 * padded), F32),
             ]
-            both = [jnp.concatenate(bias, axis=1), up_0[side] + up_1[side]]
+            both = [jnp.concatenate(bias, axis=1), sum(ref[side] for ref in ups)]
             bias_ref[2 * side : 2 * side + 2] = jnp.concatenate(both, axis=0)
 
     return launch(
         body,
         "small_grads",
-        [(a, None) for a in (norm_0, norm_1, late, *queries, *values, up_0, up_1)],
+        [(a, None) for a in (*norms, *lates, *queries, values, *up_sums)],
         [(shape((6, width), BF), None), (shape((4, width), F32), None)],
     )
 
@@ -821,7 +871,7 @@
     return swap(values, "group", 4, 3)
 
 
-def divide(kept, received, mine, count, fresh):
+def divide(kept, received, mine, count):
     rows, width = kept.shape
     part = rows // count
     total = len(received)
@@ -838,8 +888,29 @@
     return launch(
         body,
         "divide",
-        [(kept, None if fresh else held(rows, width))] + [(a, None) for a in received],
+        [(kept, held(rows, width))] + [(a, None) for a in received],
         [(shape((part, width), BF), held(part, width))] + [(shape((part, width), BF), None)] * (count - 1),
+        scalar=mine,
+    )
+
+
+def divide_first(kept, pieces, mine):
+    rows, width = kept.shape
+    part, size = rows // 2, rows // 4
+
+    def body(mine_ref, kept_ref, p_0, p_1, p_2, p_3, own_ref, sent_ref):
+        for k, out_ref in enumerate((own_ref, sent_ref)):
+            which = mine_ref[0] ^ k
+            for j, (low, high) in enumerate(((p_0, p_2), (p_1, p_3))):
+                at = pl.ds(pl.multiple_of(which * part + j * size, 8), size)
+                got = jnp.where(which == 0, to_float(low[...]), to_float(high[...]))
+                out_ref[j * size : (j + 1) * size] = (to_float(kept_ref[at]) + got).astype(BF)
+
+    return launch(
+        body,
+        "divide",
+        [(a, None) for a in (kept, *pieces)],
+        [(shape((part, width), BF), held(part, width)), (shape((part, width), BF), None)],
         scalar=mine,
     )
 
@@ -932,7 +1003,7 @@
 
 class ReplicaSum:
     def __init__(self, kept, received, size, first, others):
-        self.kept, self.received, self.size = kept, [received], size
+        self.kept, self.received, self.size = kept, received, size
         self.groups, bit, bits = [], 1, size.bit_length() - 1
         while bit < size:
             take = min(first if bit == 1 else others, bits)
@@ -952,8 +1023,10 @@
         _, count = self.groups[self.at]
         mine = self.mine().astype(jnp.int32)
         part = self.kept.shape[0] // count
-        if part % 8 == 0:
-            parts = divide(self.kept, self.received, mine.reshape(1), count, self.at == 0)
+        if self.at == 0:
+            parts = divide_first(self.kept, self.received, mine.reshape(1))
+        elif part % 8 == 0:
+            parts = divide(self.kept, self.received, mine.reshape(1), count)
         else:
             value = to_float(self.kept)
             for received in self.received:
@@ -1099,66 +1172,56 @@
     def attention_grads(side):
         return attention_weight_grad(
             (att_0, att_1),
-            state["branch"],
-            (state["dq_0"][side], state["dq_1"][side]),
-            state["dk"][side],
-            state["dv"][side],
+            (*state["branch"], *branches_far),
+            (dq_0, *dq_1),
+            state["dk"],
+            state["dv"],
             normed_one,
             shard,
             side,
         )
 
-    def first_grad(half_index, dtype):
-        return input_grad(
-            state[f"dq_{half_index}"], state["dk"], state["dv"], w_att, hat_one, half_index, dtype
-        )
-
+    branches_far, dq_1 = [], []
     for token in SEQUENCE:
-        if token == "W1":
-            state["sent"] = core_swap(mlp_weight_grad(normed_two, grad_near + grad_far, activated, hidden, 1))
+        if token == "W":
+            kept, *sent = mlp_weight_grads(normed_two, grad_near + grad_far, activated, hidden)
+            received = [core_swap(piece) for piece in sent]
+            state["m"] = ReplicaSum(kept, received, replicas, *MLP_GROUPS)
         elif token == "R":
             state["out"] = chip_swap(after(mlp_1, ORDER[0]))
-        elif token == "W0":
-            kept = mlp_weight_grad(normed_two, grad_near + grad_far, activated, hidden, 0)
-            state["m"] = ReplicaSum(kept, state["sent"], replicas, *MLP_GROUPS)
         elif token == "N":
-            grad_middle, branch_own, late_sums = second_norm_back(
+            grad_middle, *branch, late_sums = second_norm_back(
                 middle, back_0, grad_received, grad_own, grad_core, vectors
             )
-            state["branch"] = branch_own, chip_swap(branch_own)
+            state["branch"] = branch
+            branches_far.extend(chip_swap(piece) for piece in branch)
         elif token == "B0":
-            dq, dk_0, dv_0 = attend_back(
-                state["branch"][0], out_w, att_0, inv_0, exp_0, sides, 0, heads, None
+            dq_0, *key_sums = attend_back(
+                state["branch"], out_w, att_0, inv_0, exp_0, sides, 0, 0, heads, (), False
             )
-            state["dq_0"] = dq[0], dq[1]
-        elif token == "B1":
-            dq, dk, dv = attend_back(
-                state["branch"][1], out_w, att_1, inv_1, exp_1, sides, 1, heads, (dk_0, dv_0)
+        elif token == "B2":
+            dq, *key_sums = attend_back(
+                branches_far[:1], out_w, att_1, inv_1, exp_1, sides, 2, 0, heads, key_sums, False
             )
-            state["dq_1"], state["dk"], state["dv"] = [(a[0], a[1]) for a in (dq, dk, dv)]
-        elif token in ("B11", "B10"):
-            side = int(token[2])
-            parts = attend_back(
-                state["branch"][1], out_w, att_1, inv_1, exp_1, sides, 1, heads, (dk_0, dv_0), side
+            dq_1.append(dq)
+        elif token == "B3":
+            dq, _, _, state["dk"], state["dv"] = attend_back(
+                branches_far[1:], out_w, att_1, inv_1, exp_1, sides, 3, 1, heads, key_sums, True
             )
-            for key, part in zip(("dq_1", "dk", "dv"), parts):
-                state.setdefault(key, {})[side] = part[0]
+            dq_1.append(dq)
         elif token == "A1":
-            state["sent"] = core_swap(attention_grads(1))
+            state["sent"] = [core_swap(piece) for piece in attention_grads(1)]
         elif token == "A0":
-            state["a"] = ReplicaSum(attention_grads(0), state["sent"], replicas, *ATT_GROUPS)
+            state["a"] = ReplicaSum(attention_grads(0)[0], state["sent"], replicas, *ATT_GROUPS)
         elif token == "I1":
-            for key in ("dq_1", "dk", "dv"):
-                state[key] = state[key][0], state[key][1]
-            first_1, norm_1 = first_grad(1, BF)
+            first_1, norm_1 = input_grad(dq_1, state["dk"], state["dv"], w_att, hat_one, 1, BF)
             if RS4_EARLY:
                 first_received = chip_swap(first_1)
         elif token == "I0":
-            first_0, norm_0 = first_grad(0, F32)
+            first_0, norm_0 = input_grad([dq_0], state["dk"], state["dv"], w_att, hat_one, 0, F32)
         elif token == "G":
             wide, bias_sums = small_grads(
-                norm_0, norm_1, late_sums, (*state["dq_0"], *state["dq_1"]), state["dv"],
-                up_sum_0, up_sum_1,
+                (norm_0, norm_1), [late_sums], (dq_0, *dq_1), state["dv"], [up_sum_0, up_sum_1]
             )
             wide_received = chip_swap(wide)
             if not RS4_EARLY:
@@ -1176,12 +1239,18 @@
                 activations, core_piece, grad_middle, first_0, first_received, vectors, core
             )
             input_received = core_swap(input_sent)
+        elif token == "J":
+            while state["m"].rows is None or state["m"].at > 0:
+                advance("m")
+            state["m"].combine(join_mlp)
         else:
             advance(token)
-    for name in ("m", "a"):
-        while state[name].rows is None or state[name].at > 0:
-            advance(name)
-    state["m"].combine(join_mlp)
+    while state["a"].rows is None or state["a"].at > 0:
+        advance("a")
+    if "J" not in SEQUENCE:
+        while state["m"].rows is None or state["m"].at > 0:
+            advance("m")
+        state["m"].combine(join_mlp)
     state["a"].combine(lambda parts, mine: join_weights(parts, mine, shard, 8))
     weights, small = state["a"].rows[:4], state["a"].rows[4]
     mlp_sum = state["m"]

time: 277 us -> 269 us (0.971)
  waiting for transfers between devices: 90.4 us -> 84.5 us
  local copies, waits for them, and re-layouts: 22.1 us -> 16.7 us
  Pallas kernels: 133 us -> 136 us
    ppermute x33 -> x40, waiting for transfers between devices: 90.4 us -> 84.5 us  [swap(): return lax.ppermute(values, axis, [(i, i ^ bit) for i in range(size)])]
    unnamed x62 -> x66, local copies, waits for them, and re-layouts: 14 us -> 8.75 us
    ppermute x33 -> x40, starting transfers between devices: 28.1 us -> 27.6 us  [swap(): return lax.ppermute(values, axis, [(i, i ^ bit) for i in range(size)])]
  transfers between devices with their start and end apart: 33 -> 40, of which waited for: 15 -> 18; matrix products, arithmetic and copies ran while one was open for 2% -> 2% of each run, Pallas kernels for 39% -> 45%
where the time goes in v1:
time: 269 us; the launch traced here: 267 us
  Pallas kernels  136 us (51%)
  waiting for transfers between devices  84.5 us (31%)
  starting transfers between devices  27.6 us (10%)
  local copies, waits for them, and re-layouts  16.7 us (6%)
    pallas_call x39, Pallas kernels, launch(): pl.pallas_call(body, grid_spec=pltpu.PrefetchScalarGridSpec(num_scalar_pr...  136 us
    ppermute x40, waiting for transfers between devices, swap(): return lax.ppermute(values, axis, [(i, i ^ bit) for i in range(size)])  84.5 us
    ppermute x40, starting transfers between devices, swap(): return lax.ppermute(values, axis, [(i, i ^ bit) for i in range(size)])  27.6 us
    unnamed x66, local copies, waits for them, and re-layouts  8.75 us
  transfers between devices with their start and end apart: 40, of which 18 were waited for; matrix products, arithmetic and copies ran while one was open for 2% of the time, Pallas kernels for 45%

profile of v1, /device:TPU:0, one launch (start us, length us, event | category | flops | bytes accessed | tf_op | source)
XLA Modules:
  0.0 266.6 jit_solution(630302558078061760)
XLA Ops:
  22.9 6.6 %collective-permute-done.2.fourth = bf16[272,768]{1,0:T(8,128)(2,1)} collective-permute-done((bf16[272,768]{1,0:T(8,128)(2,1)}, bf16[272,768]{1,0:T(8,128)(2,1)}, u32[]{:S(2)}, u32[]{:S(2)}) %collective-permute-start.2) | collective-permute-done | bytes 417824 | tf_op jit(solution)/shard_map/ppermute | solution.py:859
  31.4 6.9 %project.1 = (bf16[1024,768]{1,0:T(8,128)(2,1)}, bf16[1024,768]{1,0:T(8,128)(2,1)}, bf16[2,1024,768]{2,1,0:T(8,128)(2,1)S(1)}, bf16[2,256,768]{2,1,0:T(8,128)(2,...) custom-call(s32[1]{0:T(128)} %bitcast.core_ref, f32[2,256,768]{2,1,0:T(8,128)} %own.5, ...), custom_call_target="tpu_custom_call" | custom-call | flops 8000000000 | bytes 1 | tf_op jit(solution)/shard_map/project/pallas_call | solution.py:97
  38.3 8.5 %attend_1.1 = (bf16[2,512,256]{2,1,0:T(8,128)(2,1)}, f32[2,512,256]{2,1,0:T(8,128)}, bf16[6,512,1024]{2,1,0:T(8,128)(2,1)}, bf16[512,768]{1,0:T(8,128)(2,1)S(1)}) custom-call(bf16[2,1024,768]{2,1,0:T(8,128)(2,1)S(1)} %get-tuple-element.157.sides.refs_5_.refs_4_, bf16[1024,256]{1,0:T(8,128)(2,1)S(1)} %fusion.1.marks, ...), custom_call_target="tpu_custom_call" | custom-call | flops 8000000000 | bytes 1 | tf_op jit(solution)/shard_map/attend_1/pallas_call | solution.py:97
  47.4 8.5 %attend_0.1 = (bf16[2,512,256]{2,1,0:T(8,128)(2,1)}, f32[2,512,256]{2,1,0:T(8,128)}, bf16[6,512,1024]{2,1,0:T(8,128)(2,1)}, f32[512,768]{1,0:T(8,128)S(1)}) custom-call(bf16[2,1024,768]{2,1,0:T(8,128)(2,1)S(1)} %get-tuple-element.157.sides.refs_5_.refs_4_, bf16[1024,256]{1,0:T(8,128)(2,1)S(1)} %fusion.1.marks, ...), custom_call_target="tpu_custom_call" | custom-call | flops 8000000000 | bytes 1 | tf_op jit(solution)/shard_map/attend_0/pallas_call | solution.py:97
  56.2 10.5 %collective-permute-done.6.recv_ref = bf16[512,768]{1,0:T(8,128)(2,1)S(1)} collective-permute-done((bf16[512,768]{1,0:T(8,128)(2,1)S(1)}, bf16[512,768]{1,0:T(8,128)(2,1)S(1)}, u32[]{:S(2)}, u32[]{:S(2)}) %collective-permute-start.6) | collective-permute-done | bytes 786464 | tf_op jit(solution)/shard_map/ppermute | solution.py:859
  70.4 9.5 %mlp_0.1 = (bf16[2,1024,768]{2,1,0:T(8,128)(2,1)S(1)}, bf16[2,1024,768]{2,1,0:T(8,128)(2,1)S(1)}, f32[512,768]{1,0:T(8,128)}, f32[512,768]{1,0:T(8,128)}, f32[2,1,768]{2,1,0:T(1,128)S(1)}) custom-call(bf16[512,768]{1,0:T(8,128)(2,1)S(1)} %get-tuple-element.174.n_ref.n_0, bf16[256,768]{1,0:T(8,128)(2,1)} %get-tuple-element.185.g_0, ...), custom_call_target="tpu_custom_call" | custom-call | flops 8000000000 | bytes 1 | tf_op jit(solution)/shard_map/mlp_0/pallas_call | solution.py:97
  79.9 9.3 %collective-permute-done.10.n_ref.n_1 = bf16[512,768]{1,0:T(8,128)(2,1)S(1)} collective-permute-done((bf16[512,768]{1,0:T(8,128)(2,1)S(1)}, bf16[512,768]{1,0:T(8,128)(2,1)S(1)}, u32[]{:S(2)}, u32[]{:S(2)}) %collective-permute-start.10) | collective-permute-done | bytes 786464 | tf_op jit(solution)/shard_map/ppermute | solution.py:859
  89.3 9.3 %mlp_1.1 = (bf16[2,1024,768]{2,1,0:T(8,128)(2,1)S(1)}, bf16[2,1024,768]{2,1,0:T(8,128)(2,1)S(1)}, bf16[512,768]{1,0:T(8,128)(2,1)}, bf16[512,768]{1,0:T(8,128)(2,1)}, f32[2,1,768]{2,1,0:T(1,128)S(1)}) custom-call(bf16[512,768]{1,0:T(8,128)(2,1)S(1)} %collective-permute-done.10.n_ref.n_1, ...), custom_call_target="tpu_custom_call", output_to_operand_aliasing={{0}: (6, {}), {1}: (7, {})} | custom-call | flops 8000000000 | bytes 1 | tf_op jit(solution)/shard_map/mlp_1/pallas_call | solution.py:97
  98.9 8.5 %mlp_weight_grads.1 = (bf16[1536,768]{1,0:T(8,128)(2,1)S(1)}, bf16[384,768]{1,0:T(8,128)(2,1)}, bf16[384,768]{1,0:T(8,128)(2,1)}, bf16[384,768]{1,0:T(8,128)(2,1)}, bf16[384,768]{1,0:T(8,128)(2,1)}) custom-call(bf16[512,768]{1,0:T(8,128)(2,1)S(1)} %get-tuple-element.174.n_ref.n_0, bf16[512,768]{1,0:T(8,128)(2,1)S(1)} %collective-permute-done.10.n_ref.n_1, ...), custom_call_target="tpu_custom_call" | custom-call | flops 1 | bytes 1 | tf_op jit(solution)/shard_map/mlp_weight_grads/pallas_call | solution.py:97
  117.2 5.6 %second_norm_back.1 = (f32[512,768]{1,0:T(8,128)}, bf16[256,768]{1,0:T(8,128)(2,1)S(1)}, bf16[256,768]{1,0:T(8,128)(2,1)S(1)}, f32[4,768]{1,0:T(4,128)S(1)}) custom-call(f32[512,768]{1,0:T(8,128)} %get-tuple-element.173.middle_ref, f32[512,768]{1,0:T(8,128)} %get-tuple-element.196.grad_ref, bf16[512,768]{1,0:T(8,128)(2,1)} %collective-permute-done.16.recv_ref, ...), custom_call_target="tpu_custom_call" | custom-call | flops 1 | bytes 1 | tf_op jit(solution)/shard_map/second_norm_back/pallas_call | solution.py:97
  125.4 11.5 %attend_back_0.1 = (bf16[2,512,256]{2,1,0:T(8,128)(2,1)S(1)}, f32[2,1024,256]{2,1,0:T(8,128)S(1)}, f32[2,1024,256]{2,1,0:T(8,128)S(1)}) custom-call(bf16[256,768]{1,0:T(8,128)(2,1)S(1)} %get-tuple-element.202.refs_0_.refs_2_, bf16[256,768]{1,0:T(8,128)(2,1)S(1)} %get-tuple-element.203.refs_1_.refs_3_, bf16[2,256,768]{2,1,0:T(8,128)(2,1)S(1)} %copy-done.19, ...), custom_call_target="tpu_custom_call" | custom-call | flops 14000000000 | bytes 1 | tf_op jit(solution)/shard_map/attend_back_0/pallas_call | solution.py:97
  136.9 6.4 %attend_back_2.1 = (bf16[2,256,256]{2,1,0:T(8,128)(2,1)S(1)}, f32[2,1024,256]{2,1,0:T(8,128)S(1)}, f32[2,1024,256]{2,1,0:T(8,128)S(1)}) custom-call(bf16[256,768]{1,0:T(8,128)(2,1)S(1)} %collective-permute-done.17.refs_0_.refs_4_, bf16[2,256,768]{2,1,0:T(8,128)(2,1)S(1)} %copy-done.19, ...), custom_call_target="tpu_custom_call", output_to_operand_aliasing={{1}: (6, {}), {2}: (7, {})} | custom-call | flops 1 | bytes 1 | tf_op jit(solution)/shard_map/attend_back_2/pallas_call | solution.py:97
  147.7 6.4 %attend_back_3.1 = (bf16[2,256,256]{2,1,0:T(8,128)(2,1)S(1)}, f32[2,1024,256]{2,1,0:T(8,128)S(1)}, f32[2,1024,256]{2,1,0:T(8,128)S(1)}, bf16[2,1024,256]{2,1,0:T(8,128)(2,1)S(1)}, bf16[2,1024,256]{2,1,0:T(8,128)(2,1)S(1)}) custom-call(bf16[256,768]{1,0:T(8,128)(2,1)S(1)} %collective-permute-done.20.refs_0_.refs_5_, ...), custom_call_target="tpu_custom_call", output_to_operand_aliasing={{1}: (6, {}), {2}: (7, {})} | custom-call | flops 8000000000 | bytes 1 | tf_op jit(solution)/shard_map/attend_back_3/pallas_call | solution.py:97
  154.1 3.9 %attention_sent.1 = (bf16[192,768]{1,0:T(8,128)(2,1)}, bf16[192,768]{1,0:T(8,128)(2,1)S(1)}, bf16[192,768]{1,0:T(8,128)(2,1)S(1)}, bf16[192,768]{1,0:T(8,128)(2,1)S(1)}) custom-call(bf16[2,512,256]{2,1,0:T(8,128)(2,1)} %get-tuple-element.168.refs_3_.refs_0_, bf16[2,512,256]{2,1,0:T(8,128)(2,1)} %get-tuple-element.163.refs_2_.refs_1_, ...), custom_call_target="tpu_custom_call" | custom-call | flops 1 | bytes 1 | tf_op jit(solution)/shard_map/attention_sent/pallas_call | solution.py:97
  170.0 3.4 %attention_kept.1.kept_ref = bf16[768,768]{1,0:T(8,128)(2,1)S(1)} custom-call(bf16[2,512,256]{2,1,0:T(8,128)(2,1)} %get-tuple-element.168.refs_3_.refs_0_, bf16[2,512,256]{2,1,0:T(8,128)(2,1)} %get-tuple-element.163.refs_2_.refs_1_, bf16[256,768]{1,0:T(8,128)(2,1)S(1)} %copy-done.9, bf16[256,768]{1,0:T(8,128)(2,1)S(1)} %copy-done.11, ...), custom_call_target="tpu_custom_call" | custom-call | flops 1 | bytes 1 | tf_op jit(solution)/shard_map/attention_kept/pallas_call | solution.py:97
  175.6 5.1 %collective-permute-done.21.refs_0_ = bf16[192,768]{1,0:T(8,128)(2,1)S(1)} collective-permute-done((bf16[192,768]{1,0:T(8,128)(2,1)S(1)}, bf16[192,768]{1,0:T(8,128)(2,1)S(1)}, u32[]{:S(2)}, u32[]{:S(2)}) %collective-permute-start.21) | collective-permute-done | bytes 294944 | tf_op jit(solution)/shard_map/ppermute | solution.py:859
  186.0 3.7 %input_grad_0.1 = (f32[512,768]{1,0:T(8,128)}, f32[2,768]{1,0:T(2,128)S(1)}) custom-call(bf16[2,512,256]{2,1,0:T(8,128)(2,1)S(1)} %get-tuple-element.239.refs_6_.refs_0_.refs_3_, bf16[2,1024,256]{2,1,0:T(8,128)(2,1)S(1)} %get-tuple-element.222.refs_9_.refs_2_.refs_1_, bf16[2,1024,256]{2,1,0:T(8,128)(2,1)S(1)} %get-tuple-element.223.refs_10_.refs_3_.refs_2_.refs_6_, ...), custom_call_target="tpu_custom_call" | custom-call | flops 1 | bytes 1 | tf_op jit(solution)/shard_map/input_grad_0/pallas_call | solution.py:97
  192.8 4.6 %collective-permute-done.29.refs_1_ = bf16[192,768]{1,0:T(8,128)(2,1)S(1)} collective-permute-done((bf16[192,768]{1,0:T(8,128)(2,1)S(1)}, bf16[192,768]{1,0:T(8,128)(2,1)S(1)}, u32[]{:S(2)}, u32[]{:S(2)}) %collective-permute-start.29) | collective-permute-done | bytes 294944 | tf_op jit(solution)/shard_map/ppermute | solution.py:859
  203.7 9.1 %collective-permute-done.33.refs_1_ = bf16[384,768]{1,0:T(8,128)(2,1)S(1)} collective-permute-done((bf16[384,768]{1,0:T(8,128)(2,1)S(1)}, bf16[384,768]{1,0:T(8,128)(2,1)S(1)}, u32[]{:S(2)}, u32[]{:S(2)}) %collective-permute-start.33) | collective-permute-done | bytes 589856 | tf_op jit(solution)/shard_map/ppermute | solution.py:859
  214.7 7.5 %collective-permute-done.31.refs_0_ = bf16[192,768]{1,0:T(8,128)(2,1)S(1)} collective-permute-done((bf16[192,768]{1,0:T(8,128)(2,1)S(1)}, bf16[192,768]{1,0:T(8,128)(2,1)S(1)}, u32[]{:S(2)}, u32[]{:S(2)}) %collective-permute-start.31) | collective-permute-done | bytes 294944 | tf_op jit(solution)/shard_map/ppermute | solution.py:859
  224.9 6.9 %collective-permute-done.34.refs_0_ = bf16[96,768]{1,0:T(8,128)(2,1)S(1)} collective-permute-done((bf16[96,768]{1,0:T(8,128)(2,1)S(1)}, bf16[96,768]{1,0:T(8,128)(2,1)S(1)}, u32[]{:S(2)}, u32[]{:S(2)}) %collective-permute-start.34) | collective-permute-done | bytes 147488 | tf_op jit(solution)/shard_map/ppermute | solution.py:859
  232.8 4.1 %first_norm_back.1 = (f32[2,256,768]{2,1,0:T(8,128)}, f32[256,768]{1,0:T(8,128)S(1)}) custom-call(s32[1]{0:T(128)} %bitcast.core_ref, f32[2,256,768]{2,1,0:T(8,128)} %own.5, f32[272,768]{1,0:T(8,128)} %collective-permute-done.second.core_piece, f32[512,768]{1,0:T(8,128)} %get-tuple-element.244.middle_ref, f32[512,768]{1,0:T(8,128)} %get-tuple-element.245.grad_ref, ...), custom_call_target="tpu_custom_call" | custom-call | flops 1 | bytes 1 | tf_op jit(solution)/shard_map/first_norm_back/pallas_call | solution.py:97
  243.2 6.8 %collective-permute-done.38.refs_1_ = bf16[200,768]{1,0:T(8,128)(2,1)S(1)} collective-permute-done((bf16[200,768]{1,0:T(8,128)(2,1)S(1)}, bf16[200,768]{1,0:T(8,128)(2,1)S(1)}, u32[]{:S(2)}, u32[]{:S(2)}) %collective-permute-start.38) | collective-permute-done | bytes 307232 | tf_op jit(solution)/shard_map/ppermute | solution.py:859
  255.0 7.9 %collective-permute-done.39.refs_1_ = bf16[392,768]{1,0:T(8,128)(2,1)S(1)} collective-permute-done((bf16[392,768]{1,0:T(8,128)(2,1)S(1)}, bf16[392,768]{1,0:T(8,128)(2,1)S(1)}, u32[]{:S(2)}, u32[]{:S(2)}) %collective-permute-start.39) | collective-permute-done | bytes 602144 | tf_op jit(solution)/shard_map/ppermute | solution.py:859
  (179 shorter events, 94.7 us)
Async XLA Ops:
  6.6 24.7 %collective-permute-start.3 = (bf16[1024,768]{1,0:T(8,128)(2,1)S(1)}, bf16[1024,768]{1,0:T(8,128)(2,1)S(1)}, u32[]{:S(2)}, u32[]{:S(2)}) collective-permute-start(bf16[1024,768]{1,0:T(8,128)(2,1)S(1)} %pack_attention.1.w_0.refs_4_.refs_3_), channel_id=1, source_target_pairs={{0,8},{8,0},{16,24},{24,16},{1,9},{9,1},{17,25},{25,17},{2,10},{10... | collective-permute-start | bytes 4718600 | tf_op jit(solution)/shard_map/ppermute | solution.py:859
  7.2 24.2 %collective-permute-start = (f32[272,768]{1,0:T(8,128)}, f32[272,768]{1,0:T(8,128)}, u32[]{:S(2)}, u32[]{:S(2)}) collective-permute-start(f32[272,768]{1,0:T(8,128)} %get-tuple-element.147), channel_id=1, source_target_pairs={{0,8},{8,0},{16,24},{24,16},{1,9},{9,1},{17,25},{25,17},{2,10},{10... | collective-permute-start | bytes 2506760 | tf_op jit(solution)/shard_map/ppermute | solution.py:859
  7.2 15.1 %collective-permute-start.1 = (bf16[272,768]{1,0:T(8,128)(2,1)}, bf16[272,768]{1,0:T(8,128)(2,1)}, u32[]{:S(2)}, u32[]{:S(2)}) collective-permute-start(bf16[272,768]{1,0:T(8,128)(2,1)} %get-tuple-element.155), channel_id=1, source_target_pairs={{0,16},{8,24},{16,0},{24,8},{1,17},{9,25},{17,1},{25,9},{2,18},{10... | collective-permute-start | bytes 1253384 | tf_op jit(solution)/shard_map/ppermute | solution.py:859
  10.2 19.3 %collective-permute-start.2 = (bf16[272,768]{1,0:T(8,128)(2,1)}, bf16[272,768]{1,0:T(8,128)(2,1)}, u32[]{:S(2)}, u32[]{:S(2)}) collective-permute-start(bf16[272,768]{1,0:T(8,128)(2,1)} %get-tuple-element.156), channel_id=1, source_target_pairs={{0,24},{8,16},{16,8},{24,0},{1,25},{9,17},{17,9},{25,1},{2,26},{10... | collective-permute-start | bytes 1253384 | tf_op jit(solution)/shard_map/ppermute | solution.py:859
  15.5 31.7 %collective-permute-start.4 = (bf16[256,768]{1,0:T(8,128)(2,1)}, bf16[256,768]{1,0:T(8,128)(2,1)}, u32[]{:S(2)}, u32[]{:S(2)}) collective-permute-start(bf16[256,768]{1,0:T(8,128)(2,1)} %get-tuple-element.185.g_0), channel_id=1, source_target_pairs={{0,16},{8,24},{16,0},{24,8},{1,17},{9,25},{17,1},{25,9},{2,18},{10... | collective-permute-start | bytes 1179656 | tf_op jit(solution)/shard_map/ppermute | solution.py:859
  22.4 33.5 %collective-permute-start.7 = (bf16[768,768]{1,0:T(8,128)(2,1)}, bf16[768,768]{1,0:T(8,128)(2,1)S(1)}, u32[]{:S(2)}, u32[]{:S(2)}) collective-permute-start(bf16[768,768]{1,0:T(8,128)(2,1)} %copy-done.14), channel_id=1, source_target_pairs={{0,8},{8,0},{16,24},{24,16},{1,9},{9,1},{17,25},{25,17},{2,10},{10... | collective-permute-start | bytes 3538952 | tf_op jit(solution)/shard_map/ppermute | solution.py:859
  29.4 17.9 %collective-permute-start.5 = (bf16[256,768]{1,0:T(8,128)(2,1)}, bf16[256,768]{1,0:T(8,128)(2,1)S(1)}, u32[]{:S(2)}, u32[]{:S(2)}) collective-permute-start(bf16[256,768]{1,0:T(8,128)(2,1)} %get-tuple-element.158), channel_id=1, source_target_pairs={{0,24},{8,16},{16,8},{24,0},{1,25},{9,17},{17,9},{25,1},{2,26},{10... | collective-permute-start | bytes 1179656 | tf_op jit(solution)/shard_map/ppermute | solution.py:859
  31.4 24.5 %collective-permute-start.8 = (bf16[768,768]{1,0:T(8,128)(2,1)}, bf16[768,768]{1,0:T(8,128)(2,1)S(1)}, u32[]{:S(2)}, u32[]{:S(2)}) collective-permute-start(bf16[768,768]{1,0:T(8,128)(2,1)} %copy-done.16), channel_id=1, source_target_pairs={{0,8},{8,0},{16,24},{24,16},{1,9},{9,1},{17,25},{25,17},{2,10},{10... | collective-permute-start | bytes 3538952 | tf_op jit(solution)/shard_map/ppermute | solution.py:859
  46.8 19.9 %collective-permute-start.6 = (bf16[512,768]{1,0:T(8,128)(2,1)S(1)}, bf16[512,768]{1,0:T(8,128)(2,1)S(1)}, u32[]{:S(2)}, u32[]{:S(2)}) collective-permute-start(bf16[512,768]{1,0:T(8,128)(2,1)S(1)} %get-tuple-element.166), channel_id=1, source_target_pairs={{0,16},{8,24},{16,0},{24,8},{1,17},{9,25},{17,1},{25,9},{2,18},{10... | collective-permute-start | bytes 2359304 | tf_op jit(solution)/shard_map/ppermute | solution.py:859
  47.2 23.2 %collective-permute-start.9 = (f32[256,768]{1,0:T(8,128)S(1)}, f32[256,768]{1,0:T(8,128)S(1)}, u32[]{:S(2)}, u32[]{:S(2)}) collective-permute-start(f32[256,768]{1,0:T(8,128)S(1)} %copy-done.27), channel_id=1, source_target_pairs={{0,8},{8,0},{16,24},{24,16},{1,9},{9,1},{17,25},{25,17},{2,10},{10... | collective-permute-start | bytes 2359304 | tf_op jit(solution)/shard_map/ppermute | solution.py:859
  70.1 19.2 %collective-permute-start.10 = (bf16[512,768]{1,0:T(8,128)(2,1)S(1)}, bf16[512,768]{1,0:T(8,128)(2,1)S(1)}, u32[]{:S(2)}, u32[]{:S(2)}) collective-permute-start(bf16[512,768]{1,0:T(8,128)(2,1)S(1)} %get-tuple-element.174.n_ref.n_0), channel_id=1, source_target_pairs={{0,16},{8,24},{16,0},{24,8},{1,17},{9,25},{17,1},{25,9},{2,18},{10... | collective-permute-start | bytes 2359304 | tf_op jit(solution)/shard_map/ppermute | solution.py:859
  98.6 18.6 %collective-permute-start.16 = (bf16[512,768]{1,0:T(8,128)(2,1)}, bf16[512,768]{1,0:T(8,128)(2,1)}, u32[]{:S(2)}, u32[]{:S(2)}) collective-permute-start(bf16[512,768]{1,0:T(8,128)(2,1)} %get-tuple-element.197), channel_id=1, source_target_pairs={{0,16},{8,24},{16,0},{24,8},{1,17},{9,25},{17,1},{25,9},{2,18},{10... | collective-permute-start | bytes 2359304 | tf_op jit(solution)/shard_map/ppermute | solution.py:859
  115.4 28.0 %collective-permute-start.18 = (bf16[768,768]{1,0:T(8,128)(2,1)S(1)}, bf16[768,768]{1,0:T(8,128)(2,1)S(1)}, u32[]{:S(2)}, u32[]{:S(2)}) collective-permute-start(bf16[768,768]{1,0:T(8,128)(2,1)S(1)} %get-tuple-element.213), channel_id=1, source_target_pairs={{0,1},{1,0},{2,3},{3,2},{4,5},{5,4},{6,7},{7,6},{8,9},{9,8},{10,11... | collective-permute-start | bytes 3538952 | tf_op jit(solution)/shard_map/ppermute | solution.py:859
  124.8 21.1 %collective-permute-start.20 = (bf16[256,768]{1,0:T(8,128)(2,1)S(1)}, bf16[256,768]{1,0:T(8,128)(2,1)S(1)}, u32[]{:S(2)}, u32[]{:S(2)}) collective-permute-start(bf16[256,768]{1,0:T(8,128)(2,1)S(1)} %get-tuple-element.203.refs_1_.refs_3_), channel_id=1, source_target_pairs={{0,16},{8,24},{16,0},{24,8},{1,17},{9,25},{17,1},{25,9},{2,18},{10... | collective-permute-start | bytes 1179656 | tf_op jit(solution)/shard_map/ppermute | solution.py:859
  145.9 16.3 %collective-permute-start.19 = (bf16[384,768]{1,0:T(8,128)(2,1)}, bf16[384,768]{1,0:T(8,128)(2,1)}, u32[]{:S(2)}, u32[]{:S(2)}) collective-permute-start(bf16[384,768]{1,0:T(8,128)(2,1)} %get-tuple-element.216), channel_id=1, source_target_pairs={{0,2},{1,3},{2,0},{3,1},{4,6},{5,7},{6,4},{7,5},{8,10},{9,11},{10,... | collective-permute-start | bytes 1769480 | tf_op jit(solution)/shard_map/ppermute | solution.py:859
  160.1 29.6 %collective-permute-start.15 = (bf16[512,768]{1,0:T(8,128)(2,1)}, bf16[512,768]{1,0:T(8,128)(2,1)}, u32[]{:S(2)}, u32[]{:S(2)}) collective-permute-start(bf16[512,768]{1,0:T(8,128)(2,1)} %get-tuple-element.195), channel_id=1, source_target_pairs={{0,16},{8,24},{16,0},{24,8},{1,17},{9,25},{17,1},{25,9},{2,18},{10... | collective-permute-start | bytes 2359304 | tf_op jit(solution)/shard_map/ppermute | solution.py:859
  164.4 16.3 %collective-permute-start.21 = (bf16[192,768]{1,0:T(8,128)(2,1)S(1)}, bf16[192,768]{1,0:T(8,128)(2,1)S(1)}, u32[]{:S(2)}, u32[]{:S(2)}) collective-permute-start(bf16[192,768]{1,0:T(8,128)(2,1)S(1)} %get-tuple-element.228), channel_id=1, source_target_pairs={{0,4},{1,5},{2,6},{3,7},{4,0},{5,1},{6,2},{7,3},{8,12},{9,13},{10,... | collective-permute-start | bytes 884744 | tf_op jit(solution)/shard_map/ppermute | solution.py:859
  181.8 15.6 %collective-permute-start.29 = (bf16[192,768]{1,0:T(8,128)(2,1)S(1)}, bf16[192,768]{1,0:T(8,128)(2,1)S(1)}, u32[]{:S(2)}, u32[]{:S(2)}) collective-permute-start(bf16[192,768]{1,0:T(8,128)(2,1)S(1)} %add_all.2.refs_0_), channel_id=1, source_target_pairs={{0,4},{1,5},{2,6},{3,7},{4,0},{5,1},{6,2},{7,3},{8,12},{9,13},{10,... | collective-permute-start | bytes 884744 | tf_op jit(solution)/shard_map/ppermute | solution.py:859
  181.9 19.9 %collective-permute-start.28 = (bf16[384,768]{1,0:T(8,128)(2,1)S(1)}, bf16[384,768]{1,0:T(8,128)(2,1)S(1)}, u32[]{:S(2)}, u32[]{:S(2)}) collective-permute-start(bf16[384,768]{1,0:T(8,128)(2,1)S(1)} %get-tuple-element.247), channel_id=1, source_target_pairs={{0,1},{1,0},{2,3},{3,2},{4,5},{5,4},{6,7},{7,6},{8,9},{9,8},{10,11... | collective-permute-start | bytes 1769480 | tf_op jit(solution)/shard_map/ppermute | solution.py:859
  197.4 15.3 %collective-permute-start.33 = (bf16[384,768]{1,0:T(8,128)(2,1)S(1)}, bf16[384,768]{1,0:T(8,128)(2,1)S(1)}, u32[]{:S(2)}, u32[]{:S(2)}) collective-permute-start(bf16[384,768]{1,0:T(8,128)(2,1)S(1)} %join.4.refs_0_), channel_id=1, source_target_pairs={{0,2},{1,3},{2,0},{3,1},{4,6},{5,7},{6,4},{7,5},{8,10},{9,11},{10,... | collective-permute-start | bytes 1769480 | tf_op jit(solution)/shard_map/ppermute | solution.py:859
  212.9 27.1 %collective-permute-start.36 = (bf16[768,768]{1,0:T(8,128)(2,1)S(1)}, bf16[768,768]{1,0:T(8,128)(2,1)S(1)}, u32[]{:S(2)}, u32[]{:S(2)}) collective-permute-start(bf16[768,768]{1,0:T(8,128)(2,1)S(1)} %join.5.first_ref), channel_id=1, source_target_pairs={{0,1},{1,0},{2,3},{3,2},{4,5},{5,4},{6,7},{7,6},{8,9},{9,8},{10,11... | collective-permute-start | bytes 3538952 | tf_op jit(solution)/shard_map/ppermute | solution.py:859
  214.4 18.3 %collective-permute-start.27 = (bf16[512,768]{1,0:T(8,128)(2,1)S(1)}, bf16[512,768]{1,0:T(8,128)(2,1)S(1)}, u32[]{:S(2)}, u32[]{:S(2)}) collective-permute-start(bf16[512,768]{1,0:T(8,128)(2,1)S(1)} %get-tuple-element.246), channel_id=1, source_target_pairs={{0,16},{8,24},{16,0},{24,8},{1,17},{9,25},{17,1},{25,9},{2,18},{10... | collective-permute-start | bytes 2359304 | tf_op jit(solution)/shard_map/ppermute | solution.py:859
  214.7 36.9 %collective-permute-start.26 = (f32[256,768]{1,0:T(8,128)S(1)}, f32[256,768]{1,0:T(8,128)}, u32[]{:S(2)}, u32[]{:S(2)}) collective-permute-start(f32[256,768]{1,0:T(8,128)S(1)} %get-tuple-element.243), channel_id=1, source_target_pairs={{0,8},{8,0},{16,24},{24,16},{1,9},{9,1},{17,25},{25,17},{2,10},{10... | collective-permute-start | bytes 2359304 | tf_op jit(solution)/shard_map/ppermute | solution.py:859
  236.9 16.9 %collective-permute-start.35 = (f32[256,768]{1,0:T(8,128)S(1)}, f32[256,768]{1,0:T(8,128)}, u32[]{:S(2)}, u32[]{:S(2)}) collective-permute-start(f32[256,768]{1,0:T(8,128)S(1)} %get-tuple-element.265), channel_id=1, source_target_pairs={{0,8},{8,0},{16,24},{24,16},{1,9},{9,1},{17,25},{25,17},{2,10},{10... | collective-permute-start | bytes 2359304 | tf_op jit(solution)/shard_map/ppermute | solution.py:859
  (49 other events, 452.6 us)

commit v2 on v1

--- a/solution.py
+++ b/solution.py
@@ -61,7 +61,7 @@
 
 SEQUENCE = (
     "W", "m", "R", "N", "B0", "B2", "m", "B3", "A1", "m",
-    "A0", "a", "m", "I1", "I0", "F", "m", "G", "C", "a",
+    "A0", "a", "m", "I1", "I0", "F", "a", "m", "G", "C",
     "U", "m", "a", "a", "L", "J",
 )
 COSTS = {
@@ -72,6 +72,8 @@
     "mlp_1": 8000000000,
     "attend_back_0": 14000000000,
     "attend_back_3": 8000000000,
+    "input_grad_0": 4000000000,
+    "finish_output": 4000000000,
 }
 MLP_GROUPS = (1, 1)
 ATT_GROUPS = (1, 1)

time: 269 us -> 265 us (0.985)
  Pallas kernels: 136 us -> 133 us
    pallas_call x39, Pallas kernels: 136 us -> 133 us  [launch(): pl.pallas_call(body, grid_spec=pltpu.PrefetchScalarGridSpec(num_scalar_pr...]
    unnamed x66 -> x76, local copies, waits for them, and re-layouts: 8.75 us -> 9.66 us
  transfers between devices with their start and end apart: 40 -> 40, of which waited for: 18 -> 19; matrix products, arithmetic and copies ran while one was open for 2% -> 2% of each run, Pallas kernels for 45% -> 45%
where the time goes in v2:
time: 265 us; the launch traced here: 264 us
  Pallas kernels  133 us (50%)
  waiting for transfers between devices  83.2 us (31%)
  starting transfers between devices  28.1 us (11%)
  local copies, waits for them, and re-layouts  17.6 us (7%)
    pallas_call x39, Pallas kernels, launch(): pl.pallas_call(body, grid_spec=pltpu.PrefetchScalarGridSpec(num_scalar_pr...  133 us
    ppermute x40, waiting for transfers between devices, swap(): return lax.ppermute(values, axis, [(i, i ^ bit) for i in range(size)])  83.2 us
    ppermute x40, starting transfers between devices, swap(): return lax.ppermute(values, axis, [(i, i ^ bit) for i in range(size)])  28.1 us
    unnamed x76, local copies, waits for them, and re-layouts  9.66 us
  transfers between devices with their start and end apart: 40, of which 19 were waited for; matrix products, arithmetic and copies ran while one was open for 2% of the time, Pallas kernels for 45%

profile of v2, /device:TPU:0, one launch (start us, length us, event | category | flops | bytes accessed | tf_op | source)
XLA Modules:
  0.0 263.6 jit_solution(3530028140793981790)
XLA Ops:
  23.4 6.1 %collective-permute-done.2.fourth = bf16[272,768]{1,0:T(8,128)(2,1)} collective-permute-done((bf16[272,768]{1,0:T(8,128)(2,1)}, bf16[272,768]{1,0:T(8,128)(2,1)}, u32[]{:S(2)}, u32[]{:S(2)}) %collective-permute-start.2) | collective-permute-done | bytes 417824 | tf_op jit(solution)/shard_map/ppermute | solution.py:861
  31.4 6.9 %project.1 = (bf16[1024,768]{1,0:T(8,128)(2,1)}, bf16[1024,768]{1,0:T(8,128)(2,1)}, bf16[2,1024,768]{2,1,0:T(8,128)(2,1)S(1)}, bf16[2,256,768]{2,1,0:T(8,128)(2,...) custom-call(s32[1]{0:T(128)} %bitcast.core_ref, f32[2,256,768]{2,1,0:T(8,128)} %own.5, ...), custom_call_target="tpu_custom_call" | custom-call | flops 8000000000 | bytes 1 | tf_op jit(solution)/shard_map/project/pallas_call | solution.py:99
  38.3 8.4 %attend_1.1 = (bf16[2,512,256]{2,1,0:T(8,128)(2,1)}, f32[2,512,256]{2,1,0:T(8,128)}, bf16[6,512,1024]{2,1,0:T(8,128)(2,1)}, bf16[512,768]{1,0:T(8,128)(2,1)S(1)}) custom-call(bf16[2,1024,768]{2,1,0:T(8,128)(2,1)S(1)} %get-tuple-element.156.sides.refs_5_.refs_4_, bf16[1024,256]{1,0:T(8,128)(2,1)S(1)} %fusion.1.marks, ...), custom_call_target="tpu_custom_call" | custom-call | flops 8000000000 | bytes 1 | tf_op jit(solution)/shard_map/attend_1/pallas_call | solution.py:99
  47.8 8.5 %attend_0.1 = (bf16[2,512,256]{2,1,0:T(8,128)(2,1)}, f32[2,512,256]{2,1,0:T(8,128)}, bf16[6,512,1024]{2,1,0:T(8,128)(2,1)}, f32[512,768]{1,0:T(8,128)S(1)}) custom-call(bf16[2,1024,768]{2,1,0:T(8,128)(2,1)S(1)} %get-tuple-element.156.sides.refs_5_.refs_4_, bf16[1024,256]{1,0:T(8,128)(2,1)S(1)} %fusion.1.marks, ...), custom_call_target="tpu_custom_call" | custom-call | flops 8000000000 | bytes 1 | tf_op jit(solution)/shard_map/attend_0/pallas_call | solution.py:99
  56.6 9.8 %collective-permute-done.6.recv_ref = bf16[512,768]{1,0:T(8,128)(2,1)S(1)} collective-permute-done((bf16[512,768]{1,0:T(8,128)(2,1)S(1)}, bf16[512,768]{1,0:T(8,128)(2,1)S(1)}, u32[]{:S(2)}, u32[]{:S(2)}) %collective-permute-start.6) | collective-permute-done | bytes 786464 | tf_op jit(solution)/shard_map/ppermute | solution.py:861
  69.9 8.6 %mlp_0.1 = (bf16[2,1024,768]{2,1,0:T(8,128)(2,1)S(1)}, bf16[2,1024,768]{2,1,0:T(8,128)(2,1)S(1)}, f32[512,768]{1,0:T(8,128)}, f32[512,768]{1,0:T(8,128)}, f32[2,1,768]{2,1,0:T(1,128)S(1)}) custom-call(bf16[512,768]{1,0:T(8,128)(2,1)S(1)} %get-tuple-element.173.n_ref.n_0, bf16[256,768]{1,0:T(8,128)(2,1)S(1)} %copy-done.21, ...), custom_call_target="tpu_custom_call" | custom-call | flops 8000000000 | bytes 1 | tf_op jit(solution)/shard_map/mlp_0/pallas_call | solution.py:99
  78.5 10.0 %collective-permute-done.10.n_ref.n_1 = bf16[512,768]{1,0:T(8,128)(2,1)S(1)} collective-permute-done((bf16[512,768]{1,0:T(8,128)(2,1)S(1)}, bf16[512,768]{1,0:T(8,128)(2,1)S(1)}, u32[]{:S(2)}, u32[]{:S(2)}) %collective-permute-start.10) | collective-permute-done | bytes 786464 | tf_op jit(solution)/shard_map/ppermute | solution.py:861
  88.5 8.3 %mlp_1.1 = (bf16[2,1024,768]{2,1,0:T(8,128)(2,1)S(1)}, bf16[2,1024,768]{2,1,0:T(8,128)(2,1)S(1)}, bf16[512,768]{1,0:T(8,128)(2,1)}, bf16[512,768]{1,0:T(8,128)(2,1)}, f32[2,1,768]{2,1,0:T(1,128)S(1)}) custom-call(bf16[512,768]{1,0:T(8,128)(2,1)S(1)} %collective-permute-done.10.n_ref.n_1, ...), custom_call_target="tpu_custom_call", output_to_operand_aliasing={{0}: (6, {}), {1}: (7, {})} | custom-call | flops 8000000000 | bytes 1 | tf_op jit(solution)/shard_map/mlp_1/pallas_call | solution.py:99
  97.2 7.4 %mlp_weight_grads.1 = (bf16[1536,768]{1,0:T(8,128)(2,1)S(1)}, bf16[384,768]{1,0:T(8,128)(2,1)}, bf16[384,768]{1,0:T(8,128)(2,1)}, bf16[384,768]{1,0:T(8,128)(2,1)}, bf16[384,768]{1,0:T(8,128)(2,1)}) custom-call(bf16[512,768]{1,0:T(8,128)(2,1)S(1)} %get-tuple-element.173.n_ref.n_0, bf16[512,768]{1,0:T(8,128)(2,1)S(1)} %collective-permute-done.10.n_ref.n_1, ...), custom_call_target="tpu_custom_call" | custom-call | flops 1 | bytes 1 | tf_op jit(solution)/shard_map/mlp_weight_grads/pallas_call | solution.py:99
  115.1 5.5 %second_norm_back.1 = (f32[512,768]{1,0:T(8,128)}, bf16[256,768]{1,0:T(8,128)(2,1)S(1)}, bf16[256,768]{1,0:T(8,128)(2,1)S(1)}, f32[4,768]{1,0:T(4,128)S(1)}) custom-call(f32[512,768]{1,0:T(8,128)} %get-tuple-element.172.middle_ref, f32[512,768]{1,0:T(8,128)} %get-tuple-element.195.grad_ref, bf16[512,768]{1,0:T(8,128)(2,1)} %collective-permute-done.16.recv_ref, ...), custom_call_target="tpu_custom_call" | custom-call | flops 1 | bytes 1 | tf_op jit(solution)/shard_map/second_norm_back/pallas_call | solution.py:99
  122.7 11.5 %attend_back_0.1 = (bf16[2,512,256]{2,1,0:T(8,128)(2,1)S(1)}, f32[2,1024,256]{2,1,0:T(8,128)S(1)}, f32[2,1024,256]{2,1,0:T(8,128)S(1)}) custom-call(bf16[256,768]{1,0:T(8,128)(2,1)S(1)} %get-tuple-element.201.refs_0_.refs_2_, bf16[256,768]{1,0:T(8,128)(2,1)S(1)} %get-tuple-element.202.refs_1_.refs_3_, bf16[2,256,768]{2,1,0:T(8,128)(2,1)S(1)} %copy-done.19, ...), custom_call_target="tpu_custom_call" | custom-call | flops 14000000000 | bytes 1 | tf_op jit(solution)/shard_map/attend_back_0/pallas_call | solution.py:99
  134.3 6.4 %attend_back_2.1 = (bf16[2,256,256]{2,1,0:T(8,128)(2,1)S(1)}, f32[2,1024,256]{2,1,0:T(8,128)S(1)}, f32[2,1024,256]{2,1,0:T(8,128)S(1)}) custom-call(bf16[256,768]{1,0:T(8,128)(2,1)S(1)} %collective-permute-done.17.refs_0_.refs_4_, bf16[2,256,768]{2,1,0:T(8,128)(2,1)S(1)} %copy-done.19, ...), custom_call_target="tpu_custom_call", output_to_operand_aliasing={{1}: (6, {}), {2}: (7, {})} | custom-call | flops 1 | bytes 1 | tf_op jit(solution)/shard_map/attend_back_2/pallas_call | solution.py:99
  144.8 6.4 %attend_back_3.1 = (bf16[2,256,256]{2,1,0:T(8,128)(2,1)S(1)}, f32[2,1024,256]{2,1,0:T(8,128)S(1)}, f32[2,1024,256]{2,1,0:T(8,128)S(1)}, bf16[2,1024,256]{2,1,0:T(8,128)(2,1)S(1)}, bf16[2,1024,256]{2,1,0:T(8,128)(2,1)S(1)}) custom-call(bf16[256,768]{1,0:T(8,128)(2,1)S(1)} %collective-permute-done.20.refs_0_.refs_5_, ...), custom_call_target="tpu_custom_call", output_to_operand_aliasing={{1}: (6, {}), {2}: (7, {})} | custom-call | flops 8000000000 | bytes 1 | tf_op jit(solution)/shard_map/attend_back_3/pallas_call | solution.py:99
  151.2 3.9 %attention_sent.1 = (bf16[192,768]{1,0:T(8,128)(2,1)}, bf16[192,768]{1,0:T(8,128)(2,1)S(1)}, bf16[192,768]{1,0:T(8,128)(2,1)S(1)}, bf16[192,768]{1,0:T(8,128)(2,1)S(1)}) custom-call(bf16[2,512,256]{2,1,0:T(8,128)(2,1)} %get-tuple-element.167.refs_3_.refs_0_, bf16[2,512,256]{2,1,0:T(8,128)(2,1)} %get-tuple-element.162.refs_2_.refs_1_, ...), custom_call_target="tpu_custom_call" | custom-call | flops 1 | bytes 1 | tf_op jit(solution)/shard_map/attention_sent/pallas_call | solution.py:99
  167.1 3.4 %attention_kept.1.kept_ref = bf16[768,768]{1,0:T(8,128)(2,1)S(1)} custom-call(bf16[2,512,256]{2,1,0:T(8,128)(2,1)} %get-tuple-element.167.refs_3_.refs_0_, bf16[2,512,256]{2,1,0:T(8,128)(2,1)} %get-tuple-element.162.refs_2_.refs_1_, bf16[256,768]{1,0:T(8,128)(2,1)S(1)} %copy-done.9, bf16[256,768]{1,0:T(8,128)(2,1)S(1)} %copy-done.11, ...), custom_call_target="tpu_custom_call" | custom-call | flops 1 | bytes 1 | tf_op jit(solution)/shard_map/attention_kept/pallas_call | solution.py:99
  174.2 3.6 %collective-permute-done.21.refs_0_ = bf16[192,768]{1,0:T(8,128)(2,1)S(1)} collective-permute-done((bf16[192,768]{1,0:T(8,128)(2,1)S(1)}, bf16[192,768]{1,0:T(8,128)(2,1)S(1)}, u32[]{:S(2)}, u32[]{:S(2)}) %collective-permute-start.21) | collective-permute-done | bytes 294944 | tf_op jit(solution)/shard_map/ppermute | solution.py:861
  182.0 4.2 %input_grad_0.1 = (f32[512,768]{1,0:T(8,128)}, f32[2,768]{1,0:T(2,128)S(1)}) custom-call(bf16[2,512,256]{2,1,0:T(8,128)(2,1)S(1)} %get-tuple-element.238.refs_6_.refs_0_.refs_3_, bf16[2,1024,256]{2,1,0:T(8,128)(2,1)S(1)} %get-tuple-element.221.refs_9_.refs_2_.refs_1_, bf16[2,1024,256]{2,1,0:T(8,128)(2,1)S(1)} %get-tuple-element.222.refs_10_.refs_3_.refs_2_.refs_6_, ...), custom_call_target="tpu_custom_call" | custom-call | flops 4000000000 | bytes 1 | tf_op jit(solution)/shard_map/input_grad_0/pallas_call | solution.py:99
  200.0 9.8 %collective-permute-done.33.refs_1_ = bf16[384,768]{1,0:T(8,128)(2,1)S(1)} collective-permute-done((bf16[384,768]{1,0:T(8,128)(2,1)S(1)}, bf16[384,768]{1,0:T(8,128)(2,1)S(1)}, u32[]{:S(2)}, u32[]{:S(2)}) %collective-permute-start.33) | collective-permute-done | bytes 589856 | tf_op jit(solution)/shard_map/ppermute | solution.py:861
  212.3 7.0 %collective-permute-done.29.refs_0_ = bf16[192,768]{1,0:T(8,128)(2,1)S(1)} collective-permute-done((bf16[192,768]{1,0:T(8,128)(2,1)S(1)}, bf16[192,768]{1,0:T(8,128)(2,1)S(1)}, u32[]{:S(2)}, u32[]{:S(2)}) %collective-permute-start.29) | collective-permute-done | bytes 294944 | tf_op jit(solution)/shard_map/ppermute | solution.py:861
  221.9 6.7 %collective-permute-done.34.refs_0_ = bf16[96,768]{1,0:T(8,128)(2,1)S(1)} collective-permute-done((bf16[96,768]{1,0:T(8,128)(2,1)S(1)}, bf16[96,768]{1,0:T(8,128)(2,1)S(1)}, u32[]{:S(2)}, u32[]{:S(2)}) %collective-permute-start.34) | collective-permute-done | bytes 147488 | tf_op jit(solution)/shard_map/ppermute | solution.py:861
  229.8 3.8 %first_norm_back.1 = (f32[2,256,768]{2,1,0:T(8,128)}, f32[256,768]{1,0:T(8,128)S(1)}) custom-call(s32[1]{0:T(128)} %bitcast.core_ref, f32[2,256,768]{2,1,0:T(8,128)} %own.5, f32[272,768]{1,0:T(8,128)S(1)} %copy-done.5, f32[512,768]{1,0:T(8,128)} %get-tuple-element.243.middle_ref, f32[512,768]{1,0:T(8,128)} %get-tuple-element.244.grad_ref, ...), custom_call_target="tpu_custom_call" | custom-call | flops 1 | bytes 1 | tf_op jit(solution)/shard_map/first_norm_back/pallas_call | solution.py:99
  233.6 3.4 %collective-permute-done.36.second_ref = bf16[768,768]{1,0:T(8,128)(2,1)S(1)} collective-permute-done((bf16[768,768]{1,0:T(8,128)(2,1)S(1)}, bf16[768,768]{1,0:T(8,128)(2,1)S(1)}, u32[]{:S(2)}, u32[]{:S(2)}) %collective-permute-start.36) | collective-permute-done | bytes 1179680 | tf_op jit(solution)/shard_map/ppermute | solution.py:861
  240.2 6.8 %collective-permute-done.38.refs_1_ = bf16[200,768]{1,0:T(8,128)(2,1)S(1)} collective-permute-done((bf16[200,768]{1,0:T(8,128)(2,1)S(1)}, bf16[200,768]{1,0:T(8,128)(2,1)S(1)}, u32[]{:S(2)}, u32[]{:S(2)}) %collective-permute-start.38) | collective-permute-done | bytes 307232 | tf_op jit(solution)/shard_map/ppermute | solution.py:861
  252.1 7.9 %collective-permute-done.39.refs_1_ = bf16[392,768]{1,0:T(8,128)(2,1)S(1)} collective-permute-done((bf16[392,768]{1,0:T(8,128)(2,1)S(1)}, bf16[392,768]{1,0:T(8,128)(2,1)S(1)}, u32[]{:S(2)}, u32[]{:S(2)}) %collective-permute-start.39) | collective-permute-done | bytes 602144 | tf_op jit(solution)/shard_map/ppermute | solution.py:861
  (189 shorter events, 97.9 us)
Async XLA Ops:
  6.6 24.7 %collective-permute-start.3 = (bf16[1024,768]{1,0:T(8,128)(2,1)S(1)}, bf16[1024,768]{1,0:T(8,128)(2,1)}, u32[]{:S(2)}, u32[]{:S(2)}) collective-permute-start(bf16[1024,768]{1,0:T(8,128)(2,1)S(1)} %pack_attention.1.w_0.refs_4_.refs_3_), channel_id=1, source_target_pairs={{0,8},{8,0},{16,24},{24,16},{1,9},{9,1},{17,25},{25,17},{2,10},{10... | collective-permute-start | bytes 4718600 | tf_op jit(solution)/shard_map/ppermute | solution.py:861
  7.2 24.2 %collective-permute-start = (f32[272,768]{1,0:T(8,128)}, f32[272,768]{1,0:T(8,128)S(1)}, u32[]{:S(2)}, u32[]{:S(2)}) collective-permute-start(f32[272,768]{1,0:T(8,128)} %get-tuple-element.146), channel_id=1, source_target_pairs={{0,8},{8,0},{16,24},{24,16},{1,9},{9,1},{17,25},{25,17},{2,10},{10... | collective-permute-start | bytes 2506760 | tf_op jit(solution)/shard_map/ppermute | solution.py:861
  7.2 15.6 %collective-permute-start.1 = (bf16[272,768]{1,0:T(8,128)(2,1)}, bf16[272,768]{1,0:T(8,128)(2,1)}, u32[]{:S(2)}, u32[]{:S(2)}) collective-permute-start(bf16[272,768]{1,0:T(8,128)(2,1)} %get-tuple-element.154), channel_id=1, source_target_pairs={{0,16},{8,24},{16,0},{24,8},{1,17},{9,25},{17,1},{25,9},{2,18},{10... | collective-permute-start | bytes 1253384 | tf_op jit(solution)/shard_map/ppermute | solution.py:861
  10.2 19.3 %collective-permute-start.2 = (bf16[272,768]{1,0:T(8,128)(2,1)}, bf16[272,768]{1,0:T(8,128)(2,1)}, u32[]{:S(2)}, u32[]{:S(2)}) collective-permute-start(bf16[272,768]{1,0:T(8,128)(2,1)} %get-tuple-element.155), channel_id=1, source_target_pairs={{0,24},{8,16},{16,8},{24,0},{1,25},{9,17},{17,9},{25,1},{2,26},{10... | collective-permute-start | bytes 1253384 | tf_op jit(solution)/shard_map/ppermute | solution.py:861
  16.0 31.0 %collective-permute-start.4 = (bf16[256,768]{1,0:T(8,128)(2,1)S(1)}, bf16[256,768]{1,0:T(8,128)(2,1)S(1)}, u32[]{:S(2)}, u32[]{:S(2)}) collective-permute-start(bf16[256,768]{1,0:T(8,128)(2,1)S(1)} %get-tuple-element.184.g_0), channel_id=1, source_target_pairs={{0,16},{8,24},{16,0},{24,8},{1,17},{9,25},{17,1},{25,9},{2,18},{10... | collective-permute-start | bytes 1179656 | tf_op jit(solution)/shard_map/ppermute | solution.py:861
  22.9 33.4 %collective-permute-start.7 = (bf16[768,768]{1,0:T(8,128)(2,1)}, bf16[768,768]{1,0:T(8,128)(2,1)S(1)}, u32[]{:S(2)}, u32[]{:S(2)}) collective-permute-start(bf16[768,768]{1,0:T(8,128)(2,1)} %copy-done.14), channel_id=1, source_target_pairs={{0,8},{8,0},{16,24},{24,16},{1,9},{9,1},{17,25},{25,17},{2,10},{10... | collective-permute-start | bytes 3538952 | tf_op jit(solution)/shard_map/ppermute | solution.py:861
  29.4 18.3 %collective-permute-start.5 = (bf16[256,768]{1,0:T(8,128)(2,1)}, bf16[256,768]{1,0:T(8,128)(2,1)S(1)}, u32[]{:S(2)}, u32[]{:S(2)}) collective-permute-start(bf16[256,768]{1,0:T(8,128)(2,1)} %copy-done.32), channel_id=1, source_target_pairs={{0,24},{8,16},{16,8},{24,0},{1,25},{9,17},{17,9},{25,1},{2,26},{10... | collective-permute-start | bytes 1179656 | tf_op jit(solution)/shard_map/ppermute | solution.py:861
  31.4 24.9 %collective-permute-start.8 = (bf16[768,768]{1,0:T(8,128)(2,1)}, bf16[768,768]{1,0:T(8,128)(2,1)S(1)}, u32[]{:S(2)}, u32[]{:S(2)}) collective-permute-start(bf16[768,768]{1,0:T(8,128)(2,1)} %copy-done.16), channel_id=1, source_target_pairs={{0,8},{8,0},{16,24},{24,16},{1,9},{9,1},{17,25},{25,17},{2,10},{10... | collective-permute-start | bytes 3538952 | tf_op jit(solution)/shard_map/ppermute | solution.py:861
  46.7 19.7 %collective-permute-start.6 = (bf16[512,768]{1,0:T(8,128)(2,1)S(1)}, bf16[512,768]{1,0:T(8,128)(2,1)S(1)}, u32[]{:S(2)}, u32[]{:S(2)}) collective-permute-start(bf16[512,768]{1,0:T(8,128)(2,1)S(1)} %get-tuple-element.165), channel_id=1, source_target_pairs={{0,16},{8,24},{16,0},{24,8},{1,17},{9,25},{17,1},{25,9},{2,18},{10... | collective-permute-start | bytes 2359304 | tf_op jit(solution)/shard_map/ppermute | solution.py:861
  47.7 22.2 %collective-permute-start.9 = (f32[256,768]{1,0:T(8,128)S(1)}, f32[256,768]{1,0:T(8,128)S(1)}, u32[]{:S(2)}, u32[]{:S(2)}) collective-permute-start(f32[256,768]{1,0:T(8,128)S(1)} %copy-done.31), channel_id=1, source_target_pairs={{0,8},{8,0},{16,24},{24,16},{1,9},{9,1},{17,25},{25,17},{2,10},{10... | collective-permute-start | bytes 2359304 | tf_op jit(solution)/shard_map/ppermute | solution.py:861
  69.6 18.9 %collective-permute-start.10 = (bf16[512,768]{1,0:T(8,128)(2,1)S(1)}, bf16[512,768]{1,0:T(8,128)(2,1)S(1)}, u32[]{:S(2)}, u32[]{:S(2)}) collective-permute-start(bf16[512,768]{1,0:T(8,128)(2,1)S(1)} %get-tuple-element.173.n_ref.n_0), channel_id=1, source_target_pairs={{0,16},{8,24},{16,0},{24,8},{1,17},{9,25},{17,1},{25,9},{2,18},{10... | collective-permute-start | bytes 2359304 | tf_op jit(solution)/shard_map/ppermute | solution.py:861
  96.8 18.3 %collective-permute-start.16 = (bf16[512,768]{1,0:T(8,128)(2,1)}, bf16[512,768]{1,0:T(8,128)(2,1)}, u32[]{:S(2)}, u32[]{:S(2)}) collective-permute-start(bf16[512,768]{1,0:T(8,128)(2,1)} %get-tuple-element.196), channel_id=1, source_target_pairs={{0,16},{8,24},{16,0},{24,8},{1,17},{9,25},{17,1},{25,9},{2,18},{10... | collective-permute-start | bytes 2359304 | tf_op jit(solution)/shard_map/ppermute | solution.py:861
  112.5 28.2 %collective-permute-start.18 = (bf16[768,768]{1,0:T(8,128)(2,1)S(1)}, bf16[768,768]{1,0:T(8,128)(2,1)S(1)}, u32[]{:S(2)}, u32[]{:S(2)}) collective-permute-start(bf16[768,768]{1,0:T(8,128)(2,1)S(1)} %get-tuple-element.212), channel_id=1, source_target_pairs={{0,1},{1,0},{2,3},{3,2},{4,5},{5,4},{6,7},{7,6},{8,9},{9,8},{10,11... | collective-permute-start | bytes 3538952 | tf_op jit(solution)/shard_map/ppermute | solution.py:861
  121.3 21.9 %collective-permute-start.20 = (bf16[256,768]{1,0:T(8,128)(2,1)S(1)}, bf16[256,768]{1,0:T(8,128)(2,1)S(1)}, u32[]{:S(2)}, u32[]{:S(2)}) collective-permute-start(bf16[256,768]{1,0:T(8,128)(2,1)S(1)} %get-tuple-element.202.refs_1_.refs_3_), channel_id=1, source_target_pairs={{0,16},{8,24},{16,0},{24,8},{1,17},{9,25},{17,1},{25,9},{2,18},{10... | collective-permute-start | bytes 1179656 | tf_op jit(solution)/shard_map/ppermute | solution.py:861
  143.2 16.0 %collective-permute-start.19 = (bf16[384,768]{1,0:T(8,128)(2,1)}, bf16[384,768]{1,0:T(8,128)(2,1)}, u32[]{:S(2)}, u32[]{:S(2)}) collective-permute-start(bf16[384,768]{1,0:T(8,128)(2,1)} %get-tuple-element.215), channel_id=1, source_target_pairs={{0,2},{1,3},{2,0},{3,1},{4,6},{5,7},{6,4},{7,5},{8,10},{9,11},{10,... | collective-permute-start | bytes 1769480 | tf_op jit(solution)/shard_map/ppermute | solution.py:861
  157.2 28.9 %collective-permute-start.15 = (bf16[512,768]{1,0:T(8,128)(2,1)}, bf16[512,768]{1,0:T(8,128)(2,1)}, u32[]{:S(2)}, u32[]{:S(2)}) collective-permute-start(bf16[512,768]{1,0:T(8,128)(2,1)} %get-tuple-element.194), channel_id=1, source_target_pairs={{0,16},{8,24},{16,0},{24,8},{1,17},{9,25},{17,1},{25,9},{2,18},{10... | collective-permute-start | bytes 2359304 | tf_op jit(solution)/shard_map/ppermute | solution.py:861
  161.5 16.3 %collective-permute-start.21 = (bf16[192,768]{1,0:T(8,128)(2,1)S(1)}, bf16[192,768]{1,0:T(8,128)(2,1)S(1)}, u32[]{:S(2)}, u32[]{:S(2)}) collective-permute-start(bf16[192,768]{1,0:T(8,128)(2,1)S(1)} %get-tuple-element.227), channel_id=1, source_target_pairs={{0,4},{1,5},{2,6},{3,7},{4,0},{5,1},{6,2},{7,3},{8,12},{9,13},{10,... | collective-permute-start | bytes 884744 | tf_op jit(solution)/shard_map/ppermute | solution.py:861
  172.6 16.6 %collective-permute-start.28 = (bf16[384,768]{1,0:T(8,128)(2,1)S(1)}, bf16[384,768]{1,0:T(8,128)(2,1)S(1)}, u32[]{:S(2)}, u32[]{:S(2)}) collective-permute-start(bf16[384,768]{1,0:T(8,128)(2,1)S(1)} %get-tuple-element.246), channel_id=1, source_target_pairs={{0,1},{1,0},{2,3},{3,2},{4,5},{5,4},{6,7},{7,6},{8,9},{9,8},{10,11... | collective-permute-start | bytes 1769480 | tf_op jit(solution)/shard_map/ppermute | solution.py:861
  178.8 15.6 %collective-permute-start.30 = (bf16[192,768]{1,0:T(8,128)(2,1)S(1)}, bf16[192,768]{1,0:T(8,128)(2,1)S(1)}, u32[]{:S(2)}, u32[]{:S(2)}) collective-permute-start(bf16[192,768]{1,0:T(8,128)(2,1)S(1)} %add_all.2.refs_0_), channel_id=1, source_target_pairs={{0,4},{1,5},{2,6},{3,7},{4,0},{5,1},{6,2},{7,3},{8,12},{9,13},{10,... | collective-permute-start | bytes 884744 | tf_op jit(solution)/shard_map/ppermute | solution.py:861
  194.5 15.3 %collective-permute-start.33 = (bf16[384,768]{1,0:T(8,128)(2,1)S(1)}, bf16[384,768]{1,0:T(8,128)(2,1)S(1)}, u32[]{:S(2)}, u32[]{:S(2)}) collective-permute-start(bf16[384,768]{1,0:T(8,128)(2,1)S(1)} %join.4.refs_0_), channel_id=1, source_target_pairs={{0,2},{1,3},{2,0},{3,1},{4,6},{5,7},{6,4},{7,5},{8,10},{9,11},{10,... | collective-permute-start | bytes 1769480 | tf_op jit(solution)/shard_map/ppermute | solution.py:861
  209.9 27.1 %collective-permute-start.36 = (bf16[768,768]{1,0:T(8,128)(2,1)S(1)}, bf16[768,768]{1,0:T(8,128)(2,1)S(1)}, u32[]{:S(2)}, u32[]{:S(2)}) collective-permute-start(bf16[768,768]{1,0:T(8,128)(2,1)S(1)} %join.5.first_ref), channel_id=1, source_target_pairs={{0,1},{1,0},{2,3},{3,2},{4,5},{5,4},{6,7},{7,6},{8,9},{9,8},{10,11... | collective-permute-start | bytes 3538952 | tf_op jit(solution)/shard_map/ppermute | solution.py:861
  211.5 18.3 %collective-permute-start.27 = (bf16[512,768]{1,0:T(8,128)(2,1)S(1)}, bf16[512,768]{1,0:T(8,128)(2,1)S(1)}, u32[]{:S(2)}, u32[]{:S(2)}) collective-permute-start(bf16[512,768]{1,0:T(8,128)(2,1)S(1)} %get-tuple-element.245), channel_id=1, source_target_pairs={{0,16},{8,24},{16,0},{24,8},{1,17},{9,25},{17,1},{25,9},{2,18},{10... | collective-permute-start | bytes 2359304 | tf_op jit(solution)/shard_map/ppermute | solution.py:861
  212.3 36.4 %collective-permute-start.26 = (f32[256,768]{1,0:T(8,128)S(1)}, f32[256,768]{1,0:T(8,128)}, u32[]{:S(2)}, u32[]{:S(2)}) collective-permute-start(f32[256,768]{1,0:T(8,128)S(1)} %get-tuple-element.242), channel_id=1, source_target_pairs={{0,8},{8,0},{16,24},{24,16},{1,9},{9,1},{17,25},{25,17},{2,10},{10... | collective-permute-start | bytes 2359304 | tf_op jit(solution)/shard_map/ppermute | solution.py:861
  233.6 17.3 %collective-permute-start.35 = (f32[256,768]{1,0:T(8,128)S(1)}, f32[256,768]{1,0:T(8,128)}, u32[]{:S(2)}, u32[]{:S(2)}) collective-permute-start(f32[256,768]{1,0:T(8,128)S(1)} %get-tuple-element.263), channel_id=1, source_target_pairs={{0,8},{8,0},{16,24},{24,16},{1,9},{9,1},{17,25},{25,17},{2,10},{10... | collective-permute-start | bytes 2359304 | tf_op jit(solution)/shard_map/ppermute | solution.py:861
  (54 other events, 531.7 us)
